TPU v7x, 128 devices: a whole 4x4x4 slice. The times are simulated.
128 devices in a mesh: row: 8 (over z, core), col: 16 (over x, y).
Axes of the slice: x: 4, y: 4, z: 4, core: 2. Of those that a mesh axis runs over, the one named last changes fastest.
Arguments:
- tokens: bfloat16 [2048, 4096], P('row', 'col'), may hold values from -6 to 6
- lengths: int32 [64], P('col'), may hold values from 1 to 64, as said below
- adapter_ids: int32 [64], P('col'), may hold values from 0 to 255, as said below
- adapter_place: int32 [256], replicated, may hold values from 0 to 255, as said below
- attention_qkv_weight: bfloat16 [2048, 6144], P('col', 'row'), may hold values from -0.125 to 0.125
- attention_out_weight: bfloat16 [2048, 2048], P('col', 'row'), may hold values from -0.125 to 0.125
- widen_weight: bfloat16 [2048, 8192], P('col', 'row'), may hold values from -0.125 to 0.125
- contract_weight: bfloat16 [2048, 8192], P('col', 'row'), may hold values from -0.0625 to 0.0625
- first_gain: float32 [2048], P('row'), may hold values from 0.5 to 1.5
- first_shift: float32 [2048], replicated, may hold values from -3 to 3
- second_gain: float32 [2048], replicated, may hold values from 0.5 to 1.5
- second_shift: float32 [2048], replicated, may hold values from -3 to 3
- attend_shrink: bfloat16 [256, 192, 2048], P('col', None, 'row'), may hold values from -0.125 to 0.125
- attend_expand: bfloat16 [256, 3, 64, 2048], P('col', None, None, 'row'), may hold values from -0.75 to 0.75
- output_shrink: bfloat16 [256, 64, 2048], P('col', None, 'row'), may hold values from -0.125 to 0.125
- output_expand: bfloat16 [256, 64, 2048], P('col', None, 'row'), may hold values from -0.75 to 0.75
- upward_shrink: bfloat16 [256, 64, 2048], P('col', None, 'row'), may hold values from -0.125 to 0.125
- upward_expand: bfloat16 [256, 64, 8192], P('col', None, 'row'), may hold values from -0.75 to 0.75
- downward_shrink: bfloat16 [256, 64, 8192], P('col', None, 'row'), may hold values from -0.0625 to 0.0625
- downward_expand: bfloat16 [256, 64, 2048], P('col', None, 'row'), may hold values from -0.75 to 0.75
Outputs:
- layer_out: bfloat16 [2048, 4096], P(None, 'col')
Inputs may be any that keep to these rules, and one draw needn't show every extreme that they name: `lengths`: each aligned block of 4 requests holds a prompt of exactly 64 tokens. `adapter_ids`: in each aligned block of 4 requests, at most 2 name adapters whose store positions lie in one aligned block of 16 positions, and exactly 2 do for some such block. `adapter_place`: A permutation.
All inputs are finite; a program needn't handle non-finite values.
Results may differ from a plain program's by a relative error of at most 0.024.
Values may be sent and summed in bfloat16 or wider, within the bound.
A program may use at most 128 MiB of HBM per device.

v0:
```python
import math

import jax
import jax.numpy as jnp
from jax import lax
from jax.sharding import PartitionSpec as P

D = 2048
HD = 128
CAP = 2


eps = 1e-12
lowrank_scale = 0.5


def fold_weight(shard, combine, initial):
    return combine(initial, lax.all_gather(shard, "col", axis=0, tiled=True), jnp.int32(0))


def project(shard, full_rows):
    initial = jnp.zeros((shard.shape[1], full_rows.shape[1]), jnp.float32)

    def accumulate(total, piece, start):
        return lax.dot_general(
            piece, full_rows, (((0,), (0,)), ((), ())), preferred_element_type=jnp.float32
        )

    return fold_weight(shard, accumulate, initial)


def gather_rows(shard):
    return lax.all_gather(shard, "row", axis=0, tiled=True)


def row_total(value):
    return lax.psum(value.astype(jnp.bfloat16), "row").astype(jnp.float32)


def route_tables(adapter_ids, adapter_place, stored, columns, capacity):
    total_adapters = adapter_place.shape[0]
    match = adapter_ids[:, None] == jnp.arange(total_adapters, dtype=jnp.int32)[None, :]
    position = jnp.sum(jnp.where(match, adapter_place[None, :], 0), axis=1)
    owner = position // stored
    local = position % stored
    count = adapter_ids.shape[0]
    earlier = jnp.arange(count)[None, :] < jnp.arange(count)[:, None]
    same_owner = owner[None, :] == owner[:, None]
    rank = jnp.sum(jnp.where(earlier & same_owner, 1, 0), axis=1).astype(jnp.int32)
    select = (owner[None, None, :] == jnp.arange(columns, dtype=jnp.int32)[:, None, None]) & (
        rank[None, None, :] == jnp.arange(capacity, dtype=jnp.int32)[None, :, None]
    )
    slot_ids = jnp.sum(jnp.where(select, local[None, None, :] + 1, 0), axis=2) - 1
    return (select.astype(jnp.bfloat16), slot_ids)


def expanded_base(expand, reduced):
    return jnp.einsum("ockp,ocks->opcs", expand, reduced, preferred_element_type=jnp.float32)


def expanded_combined(expand, reduced):
    columns, capacity, three, rank, width = expand.shape
    slot = reduced.shape[3]
    grouped = reduced.reshape(columns, capacity, three, rank, slot)
    part = jnp.einsum("ocjkp,ocjks->ojpcs", expand, grouped, preferred_element_type=jnp.float32)
    part = part.reshape(columns, three, width // HD, HD, capacity, slot)
    part = part.transpose(0, 2, 1, 3, 4, 5)
    return part.reshape(columns, three * width, capacity, slot)


def pack_slots(inputs, select):
    columns, capacity, requests = select.shape
    width = inputs.shape[0]
    slot = inputs.shape[1] // requests
    blocks = inputs.reshape(width, requests, slot)
    return jnp.einsum("okj,ijs->oiks", select, blocks, preferred_element_type=jnp.float32).astype(
        jnp.bfloat16
    )


def apply_slots(arrived, shrink, expand, expand_rule):
    partial_result = jnp.einsum(
        "ocki,oics->ocks", shrink, arrived, preferred_element_type=jnp.float32
    )
    reduced = row_total(partial_result).astype(jnp.bfloat16)
    return expand_rule(expand, reduced).astype(jnp.bfloat16)


def unpack_slots(returned, select):
    out_width = returned.shape[1]
    home = jnp.einsum("okj,opks->pjs", select, returned, preferred_element_type=jnp.float32)
    return home.reshape(out_width, -1)


def sent_delta(inputs, select, slot_ids, shrink_store, expand_store, expand_rule):
    packed = pack_slots(inputs, select)
    columns, width, capacity, slot = packed.shape
    arrived, arrived_ids = (
        lax.all_to_all(
            packed.reshape(columns, width, capacity * slot),
            "col",
            split_axis=0,
            concat_axis=0,
            tiled=True,
        ),
        lax.all_to_all(slot_ids, "col", split_axis=0, concat_axis=0, tiled=True),
    )
    arrived = arrived.reshape(columns, width, capacity, slot)
    safe_ids = jnp.maximum(arrived_ids, 0)
    lowrank_update = apply_slots(
        arrived,
        jnp.take(shrink_store, safe_ids, axis=0),
        jnp.take(expand_store, safe_ids, axis=0),
        expand_rule,
    )
    out_width = lowrank_update.shape[1]
    returned = lax.all_to_all(
        lowrank_update.reshape(columns, out_width, capacity * slot),
        "col",
        split_axis=0,
        concat_axis=0,
        tiled=True,
    )
    return unpack_slots(returned.reshape(columns, out_width, capacity, slot), select)


def layer_norm_shard(values, gain, shift):
    sums = row_total(jnp.stack([jnp.sum(values, axis=0), jnp.sum(values * values, axis=0)]))
    mean = sums[0] / D
    square_mean = sums[1] / D
    factor = lax.rsqrt(square_mean - mean * mean + eps)
    return (values - mean) * factor * gain[:, None] + shift[:, None]


def shards(
    tokens,
    lengths,
    adapter_ids,
    adapter_place,
    attention_qkv_weight,
    attention_out_weight,
    widen_weight,
    contract_weight,
    first_gain,
    first_shift,
    second_gain,
    second_shift,
    attend_shrink,
    attend_expand,
    output_shrink,
    output_expand,
    upward_shrink,
    upward_expand,
    downward_shrink,
    downward_expand,
):
    columns = lax.axis_size("col")
    stored = attend_shrink.shape[0]
    select, slot_ids = route_tables(adapter_ids, adapter_place, stored, columns, CAP)
    requests = adapter_ids.shape[0]
    width_portion, token_count = tokens.shape
    slot = token_count // requests
    column_offset = lax.axis_index("row") * width_portion
    stores = (
        (attend_shrink, attend_expand),
        (output_shrink, output_expand),
        (upward_shrink, upward_expand),
        (downward_shrink, downward_expand),
    )

    def adapter_contribution(number, inputs, expand_rule):
        return sent_delta(
            inputs, select, slot_ids, stores[number][0], stores[number][1], expand_rule
        )

    full_tokens = gather_rows(tokens)
    combined_parts = project(attention_qkv_weight, full_tokens)
    combined_parts = combined_parts + lowrank_scale * adapter_contribution(
        0, tokens, expanded_combined
    )
    combined_parts = combined_parts.astype(jnp.bfloat16).reshape(-1, 3, HD, requests, slot)
    query = combined_parts[:, 0]
    keys = combined_parts[:, 1]
    values = combined_parts[:, 2]
    scores = jnp.einsum(
        "hdrq,hdrk->hrqk", query, keys, preferred_element_type=jnp.float32
    ) / math.sqrt(HD)
    valid = jnp.arange(slot, dtype=jnp.int32)[None, :] < lengths[:, None]
    weights = jnp.where(valid[None, :, None, :], jnp.exp(scores), 0.0)
    probs = (weights / jnp.sum(weights, axis=3, keepdims=True)).astype(jnp.bfloat16)
    attended_context = jnp.einsum(
        "hdrk,hrqk->hdrq", values, probs, preferred_element_type=jnp.float32
    )
    attended_context = attended_context.astype(jnp.bfloat16).reshape(-1, token_count)
    full_context = gather_rows(attended_context)
    attention_mixed = project(attention_out_weight, full_context)
    attention_mixed = attention_mixed + lowrank_scale * adapter_contribution(
        1, attended_context, expanded_base
    )
    first_residual_input = tokens.astype(jnp.float32) + attention_mixed
    first_norm_output = layer_norm_shard(
        first_residual_input,
        first_gain,
        lax.dynamic_slice_in_dim(first_shift, column_offset, width_portion, 0),
    ).astype(jnp.bfloat16)
    full_first = gather_rows(first_norm_output)
    hidden_units = project(widen_weight, full_first)
    hidden_units = hidden_units + lowrank_scale * adapter_contribution(
        2, first_norm_output, expanded_base
    )
    hidden_units = jax.nn.gelu(hidden_units, approximate=True).astype(jnp.bfloat16)
    initial = jnp.zeros((D, token_count), jnp.float32)

    def place_rows(total, piece, start):
        return jnp.dot(piece, hidden_units, preferred_element_type=jnp.float32)

    partial_result = fold_weight(contract_weight, place_rows, initial)
    downward_update = adapter_contribution(3, hidden_units, expanded_base)
    own_rows = (
        lax.dynamic_slice_in_dim(partial_result, column_offset, width_portion, 0)
        + lowrank_scale * downward_update
    )
    partial_result = lax.dynamic_update_slice_in_dim(partial_result, own_rows, column_offset, 0)
    summed = row_total(partial_result)
    second_residual_input = full_first.astype(jnp.float32) + summed
    mean = jnp.mean(second_residual_input, axis=0)
    square_mean = jnp.mean(second_residual_input * second_residual_input, axis=0)
    factor = lax.rsqrt(square_mean - mean * mean + eps)
    result = (second_residual_input - mean) * factor * second_gain[:, None] + second_shift[:, None]
    return result.astype(jnp.bfloat16)


def solution(mesh):
    return jax.shard_map(
        shards,
        mesh=mesh,
        in_specs=(
            P("row", "col"),
            P("col"),
            P("col"),
            P(),
            P("col", "row"),
            P("col", "row"),
            P("col", "row"),
            P("col", "row"),
            P("row"),
            P(),
            P(),
            P(),
            P("col", None, "row"),
            P("col", None, None, "row"),
            P("col", None, "row"),
            P("col", None, "row"),
            P("col", None, "row"),
            P("col", None, "row"),
            P("col", None, "row"),
            P("col", None, "row"),
        ),
        out_specs=P(None, "col"),
        check_vma=False,
    )
```

profile of v0, /device:TPU:1, one launch (start us, length us, event | category | flops | bytes accessed | tf_op | source)
XLA Modules:
  0.0 914.7 jit_solution(4494370504113886302)
XLA Ops:
  8.6 7.6 all-to-all-start
  30.5 10.9 %all-to-all-done.1 = bf16[16,256,128]{1,2,0:T(8,128)(2,1)S(1)} async-done(((bf16[16,256,128]{1,2,0:T(8,128)(2,1)}), bf16[16,256,128]{1,2,0:T(8,128)(2,1)S(1)}, u32[]{:S(2)}, u32[]{:S(2)}) %all-to-all-start.1) | async-done | bytes 1048608 | tf_op jit(solution)/shard_map/all_to_all | solution.py:99
  56.0 58.4 %all-reduce.6.cloned.1.call-done = bf16[16,2,3,64,64]{3,4,1,2,0:T(8,128)(2,1)} async-done(((bf16[16,2,3,64,64]{3,4,1,2,0:T(8,128)(2,1)}), bf16[16,2,3,64,64]{3,4,1,2,0:T(8,128)(2,1)}) %all-reduce.6.cloned.1.call-update) | async-done | bytes 786448 | tf_op jit(solution)/shard_map/psum | solution.py:37
  114.4 5.2 convert_bitcast_fusion.1
  119.5 5.5 convert_element_type.122
  125.0 9.3 %copy.256 = bf16[16,3,2,128,2,64]{3,1,2,5,4,0:T(4,128)(2,1)} copy(bf16[16,3,2,128,2,64]{3,2,5,4,1,0:T(2,128)(2,1)} %convert_element_type.122) | data formatting | bytes 6291456 | tf_op jit(solution)/shard_map/convert_element_type | solution.py:86
  134.3 8.9 convert_element_type.124
  143.2 7.2 all-to-all-start.2
  151.0 39.0 %all-to-all-done.2 = bf16[16,768,128]{1,2,0:T(8,128)(2,1)} async-done(((bf16[16,768,128]{1,2,0:T(8,128)(2,1)}), bf16[16,768,128]{1,2,0:T(8,128)(2,1)}, u32[]{:S(2)}, u32[]{:S(2)}) %all-to-all-start.2) | async-done | bytes 3145760 | tf_op jit(solution)/shard_map/all_to_all | solution.py:117
  195.1 26.2 %all-gather.8.cloned.1.call-done = bf16[2048,768]{1,0:T(8,128)(2,1)} async-done(((bf16[128,768]{1,0:T(8,128)(2,1)}), bf16[2048,768]{1,0:T(8,128)(2,1)}) %all-gather.8.cloned.1.call-update) | async-done | bytes 3145744 | tf_op jit(solution)/shard_map/all_gather | solution.py:18
  239.5 13.5 %all-to-all-done.3 = bf16[16,256,128]{1,2,0:T(8,128)(2,1)} async-done(((bf16[16,256,128]{1,2,0:T(8,128)(2,1)}), bf16[16,256,128]{1,2,0:T(8,128)(2,1)}, u32[]{:S(2)}, u32[]{:S(2)}) %all-to-all-start.3) | async-done | bytes 1048608 | tf_op jit(solution)/shard_map/all_to_all | solution.py:99
  259.0 56.2 %all-reduce.8.cloned.1.call-done = bf16[16,2,64,64]{3,2,1,0:T(8,128)(2,1)} async-done(((bf16[16,2,64,64]{3,2,1,0:T(8,128)(2,1)}), bf16[16,2,64,64]{3,2,1,0:T(8,128)(2,1)}) %all-reduce.8.cloned.1.call-update) | async-done | bytes 262160 | tf_op jit(solution)/shard_map/psum | solution.py:37
  317.7 6.7 all-to-all-start.4
  325.1 13.9 %all-to-all-done.4 = bf16[16,256,128]{1,2,0:T(8,128)(2,1)S(1)} async-done(((bf16[16,256,128]{1,2,0:T(8,128)(2,1)}), bf16[16,256,128]{1,2,0:T(8,128)(2,1)S(1)}, u32[]{:S(2)}, u32[]{:S(2)}) %all-to-all-start.4) | async-done | bytes 1048608 | tf_op jit(solution)/shard_map/all_to_all | solution.py:117
  339.8 24.0 %all-gather.14.cloned.1.call-done = bf16[2048,256]{1,0:T(8,128)(2,1)} async-done(((bf16[128,256]{1,0:T(8,128)(2,1)}), bf16[2048,256]{1,0:T(8,128)(2,1)}) %all-gather.14.cloned.1.call-update) | async-done | bytes 1048592 | tf_op jit(solution)/shard_map/all_gather | solution.py:18
  363.8 26.6 %all-gather.12.cloned.1.call-done = bf16[2048,256]{0,1:T(8,128)(2,1)} async-done(((bf16[256,256]{0,1:T(8,128)(2,1)}), bf16[2048,256]{0,1:T(8,128)(2,1)}) %all-gather.12.cloned.1.call-update) | async-done | bytes 1048592 | tf_op jit(solution)/shard_map/all_gather | solution.py:33
  392.5 12.2 %psum.44 = bf16[2,256]{1,0:T(2,128)(2,1)S(1)} all-reduce(bf16[2,256]{1,0:T(2,128)(2,1)S(1)} %pad_maximum_fusion), channel_id=1, replica_groups=mesh['row'=8,'col'=16] {'row'}, use_global_device_ids=true, to_apply=%region_8.10 | all-reduce | flops 512 | bytes 2048 | tf_op jit(solution)/shard_map/psum | solution.py:37
  407.0 6.6 all-to-all-start.5
  415.2 12.9 %all-to-all-done.5 = bf16[16,256,128]{1,2,0:T(8,128)(2,1)} async-done(((bf16[16,256,128]{1,2,0:T(8,128)(2,1)}), bf16[16,256,128]{1,2,0:T(8,128)(2,1)}, u32[]{:S(2)}, u32[]{:S(2)}) %all-to-all-start.5) | async-done | bytes 1048608 | tf_op jit(solution)/shard_map/all_to_all | solution.py:99
  434.6 56.3 %all-reduce.10.cloned.1.call-done = bf16[16,2,64,64]{3,2,1,0:T(8,128)(2,1)} async-done(((bf16[16,2,64,64]{3,2,1,0:T(8,128)(2,1)}), bf16[16,2,64,64]{3,2,1,0:T(8,128)(2,1)}) %all-reduce.10.cloned.1.call-update) | async-done | bytes 262160 | tf_op jit(solution)/shard_map/psum | solution.py:37
  491.0 5.7 fusion.15
  496.6 6.6 all-to-all-start.6
  504.0 55.8 %all-to-all-done.6 = bf16[16,1024,128]{1,2,0:T(8,128)(2,1)} async-done(((bf16[16,1024,128]{1,2,0:T(8,128)(2,1)}), bf16[16,1024,128]{1,2,0:T(8,128)(2,1)}, u32[]{:S(2)}, u32[]{:S(2)}) %all-to-all-start.6) | async-done | bytes 4194336 | tf_op jit(solution)/shard_map/all_to_all | solution.py:117
  565.1 27.1 %all-gather.18.cloned.1.call-done = bf16[2048,1024]{1,0:T(8,128)(2,1)} async-done(((bf16[128,1024]{1,0:T(8,128)(2,1)}), bf16[2048,1024]{1,0:T(8,128)(2,1)}) %all-gather.18.cloned.1.call-update) | async-done | bytes 4194320 | tf_op jit(solution)/shard_map/all_gather | solution.py:18
  592.1 31.9 %all-gather.16.cloned.1.call-done = bf16[2048,256]{0,1:T(8,128)(2,1)} async-done(((bf16[256,256]{0,1:T(8,128)(2,1)}), bf16[2048,256]{0,1:T(8,128)(2,1)}) %all-gather.16.cloned.1.call-update) | async-done | bytes 1048592 | tf_op jit(solution)/shard_map/all_gather | solution.py:33
  633.9 6.7 all-to-all-start.7
  643.5 52.7 %all-to-all-done.7 = bf16[16,1024,128]{1,2,0:T(8,128)(2,1)} async-done(((bf16[16,1024,128]{1,2,0:T(8,128)(2,1)}), bf16[16,1024,128]{1,2,0:T(8,128)(2,1)}, u32[]{:S(2)}, u32[]{:S(2)}) %all-to-all-start.7) | async-done | bytes 4194336 | tf_op jit(solution)/shard_map/all_to_all | solution.py:99
  696.2 5.6 fusion.38
  703.2 66.3 %all-reduce.12.cloned.1.call-done = bf16[16,2,64,64]{3,2,1,0:T(8,128)(2,1)} async-done(((bf16[16,2,64,64]{3,2,1,0:T(8,128)(2,1)}), bf16[16,2,64,64]{3,2,1,0:T(8,128)(2,1)}) %all-reduce.12.cloned.1.call-update) | async-done | bytes 262160 | tf_op jit(solution)/shard_map/psum | solution.py:37
  772.1 6.5 all-to-all-start.8
  778.7 50.9 %all-gather.20.cloned.1.call-done = bf16[2048,1024]{1,0:T(8,128)(2,1)} async-done(((bf16[128,1024]{1,0:T(8,128)(2,1)}), bf16[2048,1024]{1,0:T(8,128)(2,1)}) %all-gather.20.cloned.1.call-update) | async-done | bytes 4194320 | tf_op jit(solution)/shard_map/all_gather | solution.py:18
  839.8 60.9 %all-reduce.14.cloned.1.call-done = bf16[2048,256]{0,1:T(8,128)(2,1)} async-done(((bf16[2048,256]{0,1:T(8,128)(2,1)}), bf16[2048,256]{0,1:T(8,128)(2,1)}) %all-reduce.14.cloned.1.call-update) | async-done | bytes 1048592 | tf_op jit(solution)/shard_map/psum | solution.py:37
  (143 shorter events, 116.9 us)
Async XLA Ops:
  6.5 425.2 %copy-start = (bf16[16,64,1024]{2,1,0:T(8,128)(2,1)S(1)}, bf16[16,64,1024]{2,1,0:T(8,128)(2,1)}, u32[]{:S(2)}) copy-start(bf16[16,64,1024]{2,1,0:T(8,128)(2,1)} %param.41) | copy-start | bytes 6291460
  8.6 14.0 %all-to-all-start = ((s32[16,1,2]{2,1,0:T(1,128)}), s32[16,1,2]{2,1,0:T(1,128)S(1)}, u32[]{:S(2)}, u32[]{:S(2)}) async-start(s32[16,1,2]{2,1,0:T(1,128)} %copy.149), calls=%async_computation | async-start | bytes 16384 | tf_op jit(solution)/shard_map/all_to_all | solution.py:106
  22.6 18.7 %all-to-all-start.1 = ((bf16[16,256,128]{1,2,0:T(8,128)(2,1)}), bf16[16,256,128]{1,2,0:T(8,128)(2,1)S(1)}, u32[]{:S(2)}, u32[]{:S(2)}) async-start(bf16[16,256,128]{1,2,0:T(8,128)(2,1)} %copy.154), calls=%async_computation.1 | async-start | bytes 2097152 | tf_op jit(solution)/shard_map/all_to_all | solution.py:99
  26.3 88.1 %all-reduce.6.cloned.1.call-start = ((), (), s32[]{:S(2)}) async-start(), calls=%async_computation.11 | async-start | bytes 3145728 | tf_op jit(solution)/shard_map/psum | solution.py:37
  50.6 144.5 %all-gather.10.cloned.1.call-start = ((), (), s32[]{:S(2)}) async-start(), calls=%async_computation.10 | async-start | bytes 1179648 | tf_op jit(solution)/shard_map/all_gather | solution.py:33
  51.4 169.9 %all-gather.8.cloned.1.call-start = ((), (), s32[]{:S(2)}) async-start(), calls=%async_computation.9 | async-start | bytes 3342336 | tf_op jit(solution)/shard_map/all_gather | solution.py:18
  143.2 7.2 copy-start.15
  143.2 46.8 %all-to-all-start.2 = ((bf16[16,768,128]{1,2,0:T(8,128)(2,1)}), bf16[16,768,128]{1,2,0:T(8,128)(2,1)}, u32[]{:S(2)}, u32[]{:S(2)}) async-start(bf16[16,768,128]{1,2,0:T(8,128)(2,1)} %convert_element_type.124), calls=%async_computation.2 | async-start | bytes 6291456 | tf_op jit(solution)/shard_map/all_to_all | solution.py:117
  230.8 7.0 copy-start.5
  233.2 19.8 %all-to-all-start.3 = ((bf16[16,256,128]{1,2,0:T(8,128)(2,1)}), bf16[16,256,128]{1,2,0:T(8,128)(2,1)}, u32[]{:S(2)}, u32[]{:S(2)}) async-start(bf16[16,256,128]{1,2,0:T(8,128)(2,1)} %bitcast.27), calls=%async_computation.3 | async-start | bytes 2097152 | tf_op jit(solution)/shard_map/all_to_all | solution.py:99
  237.5 77.6 %all-reduce.8.cloned.1.call-start = ((), (), s32[]{:S(2)}) async-start(), calls=%async_computation.14 | async-start | bytes 1048576 | tf_op jit(solution)/shard_map/psum | solution.py:37
  255.8 107.9 %all-gather.14.cloned.1.call-start = ((), (), s32[]{:S(2)}) async-start(), calls=%async_computation.13 | async-start | bytes 1114112 | tf_op jit(solution)/shard_map/all_gather | solution.py:18
  256.4 134.0 %all-gather.12.cloned.1.call-start = ((), (), s32[]{:S(2)}) async-start(), calls=%async_computation.12 | async-start | bytes 1179648 | tf_op jit(solution)/shard_map/all_gather | solution.py:33
  317.7 87.1 %copy-start.14 = (f32[256]{0:T(256)S(1)}, f32[256]{0:T(256)}, u32[]{:S(2)}) copy-start(f32[256]{0:T(256)} %param.32) | copy-start | bytes 3076
  317.7 21.3 %all-to-all-start.4 = ((bf16[16,256,128]{1,2,0:T(8,128)(2,1)}), bf16[16,256,128]{1,2,0:T(8,128)(2,1)S(1)}, u32[]{:S(2)}, u32[]{:S(2)}) async-start(bf16[16,256,128]{1,2,0:T(8,128)(2,1)} %bitcast.31), calls=%async_computation.4 | async-start | bytes 2097152 | tf_op jit(solution)/shard_map/all_to_all | solution.py:117
  392.5 21.2 %copy-start.6 = (bf16[16,64,256]{2,1,0:T(8,128)(2,1)S(1)}, bf16[16,64,256]{2,1,0:T(8,128)(2,1)}, u32[]{:S(2)}) copy-start(bf16[16,64,256]{2,1,0:T(8,128)(2,1)} %param.40) | copy-start | bytes 1572868
  404.9 10.4 %copy-start.8 = (bf16[256,256]{0,1:T(8,128)(2,1)}, bf16[256,256]{0,1:T(8,128)(2,1)S(1)}, u32[]{:S(2)}) copy-start(bf16[256,256]{0,1:T(8,128)(2,1)S(1)} %add_convert_fusion.1) | copy-start | bytes 393220
  407.0 21.1 %all-to-all-start.5 = ((bf16[16,256,128]{1,2,0:T(8,128)(2,1)}), bf16[16,256,128]{1,2,0:T(8,128)(2,1)}, u32[]{:S(2)}, u32[]{:S(2)}) async-start(bf16[16,256,128]{1,2,0:T(8,128)(2,1)} %bitcast.44), calls=%async_computation.5 | async-start | bytes 2097152 | tf_op jit(solution)/shard_map/all_to_all | solution.py:99
  413.6 77.4 %all-reduce.10.cloned.1.call-start = ((), (), s32[]{:S(2)}) async-start(), calls=%async_computation.17 | async-start | bytes 1048576 | tf_op jit(solution)/shard_map/psum | solution.py:37
  431.0 161.1 %all-gather.18.cloned.1.call-start = ((), (), s32[]{:S(2)}) async-start(), calls=%async_computation.16 | async-start | bytes 4456448 | tf_op jit(solution)/shard_map/all_gather | solution.py:18
  496.6 63.1 %all-to-all-start.6 = ((bf16[16,1024,128]{1,2,0:T(8,128)(2,1)}), bf16[16,1024,128]{1,2,0:T(8,128)(2,1)}, u32[]{:S(2)}, u32[]{:S(2)}) async-start(bf16[16,1024,128]{1,2,0:T(8,128)(2,1)} %bitcast.185), calls=%async_computation.6 | async-start | bytes 8388608 | tf_op jit(solution)/shard_map/all_to_all | solution.py:117
  503.2 120.8 %all-gather.16.cloned.1.call-start = ((), (), s32[]{:S(2)}) async-start(), calls=%async_computation.15 | async-start | bytes 1179648 | tf_op jit(solution)/shard_map/all_gather | solution.py:33
  633.9 62.3 %all-to-all-start.7 = ((bf16[16,1024,128]{1,2,0:T(8,128)(2,1)}), bf16[16,1024,128]{1,2,0:T(8,128)(2,1)}, u32[]{:S(2)}, u32[]{:S(2)}) async-start(bf16[16,1024,128]{1,2,0:T(8,128)(2,1)} %bitcast.186), calls=%async_computation.7 | async-start | bytes 8388608 | tf_op jit(solution)/shard_map/all_to_all | solution.py:99
  640.6 129.0 %all-reduce.12.cloned.1.call-start = ((), (), s32[]{:S(2)}) async-start(), calls=%async_computation.19 | async-start | bytes 1048576 | tf_op jit(solution)/shard_map/psum | solution.py:37
  701.8 127.8 %all-gather.20.cloned.1.call-start = ((), (), s32[]{:S(2)}) async-start(), calls=%async_computation.18 | async-start | bytes 4456448 | tf_op jit(solution)/shard_map/all_gather | solution.py:18
  702.6 127.0 %copy-start.11 = (bf16[1024,256]{0,1:T(8,128)(2,1)S(1)}, bf16[1024,256]{0,1:T(8,128)(2,1)}, u32[]{:S(2)}) copy-start(bf16[1024,256]{0,1:T(8,128)(2,1)} %copy-done.10) | copy-start | bytes 1572868
  772.1 62.5 %all-to-all-start.8 = ((bf16[16,256,128]{1,2,0:T(8,128)(2,1)}), bf16[16,256,128]{1,2,0:T(8,128)(2,1)S(1)}, u32[]{:S(2)}, u32[]{:S(2)}) async-start(bf16[16,256,128]{1,2,0:T(8,128)(2,1)} %bitcast.64), calls=%async_computation.8 | async-start | bytes 2097152 | tf_op jit(solution)/shard_map/all_to_all | solution.py:117
  778.6 122.1 %all-reduce.14.cloned.1.call-start = ((), (), s32[]{:S(2)}) async-start(), calls=%async_computation.20 | async-start | bytes 2097152 | tf_op jit(solution)/shard_map/psum | solution.py:37
  835.6 65.1 %copy-start.3 = (bf16[2048,256]{0,1:T(8,128)(2,1)S(1)}, bf16[2048,256]{0,1:T(8,128)(2,1)}, u32[]{:S(2)}) copy-start(bf16[2048,256]{0,1:T(8,128)(2,1)} %all-gather.16.cloned.1.call-done) | copy-start | bytes 3145732
  838.7 64.0 %copy-start.12 = (f32[2048]{0:T(1024)S(1)}, f32[2048]{0:T(1024)}, u32[]{:S(2)}) copy-start(f32[2048]{0:T(1024)} %param.35) | copy-start | bytes 24580
  838.7 64.0 %copy-start.13 = (f32[2048]{0:T(1024)S(1)}, f32[2048]{0:T(1024)}, u32[]{:S(2)}) copy-start(f32[2048]{0:T(1024)} %param.34) | copy-start | bytes 24580
  900.7 7.0 copy-start.1
  (5 other events, 21.3 us)
Sparse Core Ops, SparseCore 0:
  50.7 63.5 all-reduce.5
  116.1 25.1 all-gather.9
  143.4 77.8 all-gather.7
  255.9 59.1 all-reduce.7
  317.1 46.5 all-gather.13
  365.3 25.0 all-gather.11
  431.1 59.7 all-reduce.9
  493.1 98.9 all-gather.17
  593.8 30.1 all-gather.15
  701.9 67.5 all-reduce.11
  771.7 57.8 all-gather.19
  840.0 60.7 all-reduce.13
where the time goes:
time: 926 us; the launch traced here: 915 us
  waiting for transfers between devices  691 us (75%)
  local copies, waits for them, and re-layouts  71.5 us (8%)
  matrix products  60.5 us (7%)
  starting transfers between devices  56.7 us (6%)
  between operations  14.3 us (2%)
  blocking collectives  12.2 us (1%)
    psum x5, waiting for transfers between devices, row_total(): return lax.psum(value.astype(jnp.bfloat16), 'row').astype(jnp.float32)  298 us
    all_gather x4, waiting for transfers between devices, fold_weight(): lax.all_gather(shard, 'col', axis=0, tiled=True)  128 us
    all_to_all x4, waiting for transfers between devices, sent_delta(): lax.all_to_all(lowrank_update.reshape(columns, out_width, capacity * slot...  109 us
    all_to_all x4, waiting for transfers between devices, sent_delta(): lax.all_to_all(packed.reshape(columns, width, capacity * slot), 'col', sp...  90 us
    all_gather x3, waiting for transfers between devices, gather_rows(): return lax.all_gather(shard, 'row', axis=0, tiled=True)  58.5 us
    all_to_all x4, starting transfers between devices, sent_delta(): lax.all_to_all(lowrank_update.reshape(columns, out_width, capacity * slot...  26.9 us
    convert_element_type x3, local copies, waits for them, and re-layouts, apply_slots(): return expand_rule(expand, reduced).astype(jnp.bfloat16)  23.7 us
    all_to_all x4, starting transfers between devices, sent_delta(): lax.all_to_all(packed.reshape(columns, width, capacity * slot), 'col', sp...  21.3 us
  transfers between devices with their start and end apart: 21, of which 19 were waited for; matrix products, arithmetic and copies ran while one was open for 9% of the time, Pallas kernels for 0%

commit v1 on v0

v1 whole, which is shorter than its diff:
```python
import functools
import math

import jax
import jax.numpy as jnp
from jax import lax
from jax.experimental import pallas as pl
from jax.experimental.pallas import tpu as pltpu
from jax.sharding import PartitionSpec as P

D = 2048
HD = 128
SLOT = 64
RANK = 64
GRP = 4
TOK = GRP * SLOT
K = 12
REQ_COL = 4

eps = 1e-12
lowrank_scale = 0.5

MESH = pl.DeviceIdType.MESH
HBM = pl.BlockSpec(memory_space=pl.ANY)
NT = (((1,), (1,)), ((), ()))
f32 = jnp.float32
bf16 = jnp.bfloat16


def dot(a, b):
    return jnp.dot(a, b, preferred_element_type=f32)


def dot_nt(a, b):
    return lax.dot_general(a, b, NT, preferred_element_type=f32)


def greet(peers):
    barrier = pltpu.get_barrier_semaphore()
    for peer in peers:
        pl.semaphore_signal(barrier, inc=1, device_id=peer, device_id_type=MESH)
    pl.semaphore_wait(barrier, len(peers))


class Sender:
    def __init__(self, send_sem, recv_sem):
        self.send_sem, self.recv_sem = send_sem, recv_sem
        self.copies = []

    def start(self, src, dst, peer):
        i = len(self.copies)
        copy = pltpu.make_async_remote_copy(
            src_ref=src,
            dst_ref=dst,
            send_sem=self.send_sem.at[i],
            recv_sem=self.recv_sem.at[i],
            device_id=peer,
            device_id_type=MESH,
        )
        copy.start()
        self.copies.append(copy)
        return copy


def row_place():
    row = lax.axis_index("row")
    col = lax.axis_index("col")
    z, core = row // 2, row % 2
    return row, col, z, core


def ring_gather(buf, row, col, z, core, sender):
    half = buf.shape[1] // 2
    up, down = (z + 1) % 4, (z + 3) % 4
    far = (z + 2) % 4

    def part(zz, h):
        return buf.at[zz * 2 + core, pl.ds(h * half, half)]

    def dev(zz):
        return (zz * 2 + core, col)

    partner = (z * 2 + 1 - core, col)
    a0 = sender.start(part(z, 0), part(z, 0), dev(up))
    b1 = sender.start(part(z, 1), part(z, 1), dev(down))
    a1 = sender.start(part(z, 1), part(z, 1), dev(up))
    b0 = sender.start(part(z, 0), part(z, 0), dev(down))
    own = sender.start(buf.at[row], buf.at[row], partner)
    rest = [own]

    def across(zz, h):
        rest.append(sender.start(part(zz, h), part(zz, h), partner))

    a0.wait_recv()
    r0 = sender.start(part(down, 0), part(down, 0), dev(up))
    across(down, 0)
    b1.wait_recv()
    r1 = sender.start(part(up, 1), part(up, 1), dev(down))
    across(up, 1)
    a1.wait_recv()
    across(down, 1)
    b0.wait_recv()
    across(up, 0)
    r0.wait_recv()
    across(far, 0)
    r1.wait_recv()
    across(far, 1)
    for copy in rest:
        copy.wait_recv()


def row_neighbours(col, z, core):
    return [
        (((z + 1) % 4) * 2 + core, col),
        (((z + 3) % 4) * 2 + core, col),
        (z * 2 + 1 - core, col),
    ]


def row_gather_kernel(in_ref, out_ref, send_sem, recv_sem):
    row, col, z, core = row_place()
    greet(row_neighbours(col, z, core))
    sender = Sender(send_sem, recv_sem)
    ring_gather(out_ref, row, col, z, core, sender)
    for copy in sender.copies:
        copy.wait_send()


def row_gather(buf, cid):
    return pl.pallas_call(
        row_gather_kernel,
        out_shape=jax.ShapeDtypeStruct(buf.shape, buf.dtype),
        in_specs=[HBM],
        out_specs=HBM,
        scratch_shapes=[pltpu.SemaphoreType.DMA((13,)), pltpu.SemaphoreType.DMA((13,))],
        input_output_aliases={0: 0},
        compiler_params=pltpu.CompilerParams(collective_id=cid, has_side_effects=True),
        name="row_gather",
    )(buf)


def stat_gather_kernel(in_ref, out_ref, send_sem, recv_sem, own_sem):
    row = lax.axis_index("row")
    col = lax.axis_index("col")
    peers = [((row + i) % 8, col) for i in range(1, 8)]
    own = pltpu.make_async_copy(in_ref, out_ref.at[row], own_sem)
    own.start()
    greet(peers)
    sender = Sender(send_sem, recv_sem)
    for peer in peers:
        sender.start(in_ref, out_ref.at[row], peer)
    own.wait()
    for copy in sender.copies:
        copy.wait()


def stat_gather(part, cid):
    return pl.pallas_call(
        stat_gather_kernel,
        out_shape=jax.ShapeDtypeStruct((8,) + part.shape, part.dtype),
        in_specs=[pl.BlockSpec(memory_space=pltpu.VMEM)],
        out_specs=pl.BlockSpec(memory_space=pltpu.VMEM),
        scratch_shapes=[
            pltpu.SemaphoreType.DMA((7,)),
            pltpu.SemaphoreType.DMA((7,)),
            pltpu.SemaphoreType.DMA,
        ],
        compiler_params=pltpu.CompilerParams(collective_id=cid, has_side_effects=True),
        name="stat_gather",
    )(part)


def torus_gather(src, dst, row, x, y, sender):
    rows = src.shape[0]
    half, quarter = rows // 2, rows // 4

    def step(p, d):
        return (p + d) % 4

    flows = []
    for first in (0, 1):
        base = first * half

        def at(a, b, first=first):
            return (a * 4 + b) if first == 0 else (b * 4 + a)

        p, q = (x, y) if first == 0 else (y, x)

        def dev(a, b, at=at):
            return (row, at(a, b))

        def blk(a, b, lo, n, at=at, base=base):
            return dst.at[at(a, b), pl.ds(base + lo, n)]

        own = src.at[pl.ds(base, half)]
        flows.append((p, q, dev, blk, own))

    state = []
    for p, q, dev, blk, own in flows:
        here = blk(p, q, 0, half)
        a = sender.start(own, here, dev(step(p, 1), q))
        b = sender.start(own, here, dev(step(p, 3), q))
        c = sender.start(own, here, dev(p, step(q, 1)))
        d = sender.start(own, here, dev(p, step(q, 3)))
        state.append([a, b, [(p, c, d)]])
    yield
    relays = []
    for (p, q, dev, blk, own), st in zip(flows, state):
        a, b, second = st
        lo, hi = step(p, 3), step(p, 1)
        a.wait_recv()
        v = blk(lo, q, 0, quarter)
        r0 = sender.start(v, v, dev(step(p, 1), q))
        v = blk(lo, q, 0, half)
        second.append(
            (lo, sender.start(v, v, dev(p, step(q, 1))), sender.start(v, v, dev(p, step(q, 3))))
        )
        b.wait_recv()
        v = blk(hi, q, quarter, quarter)
        r1 = sender.start(v, v, dev(step(p, 3), q))
        v = blk(hi, q, 0, half)
        second.append(
            (hi, sender.start(v, v, dev(p, step(q, 1))), sender.start(v, v, dev(p, step(q, 3))))
        )
        st.append((r0, r1))
    yield
    for (p, q, dev, blk, own), st in zip(flows, state):
        second, (r0, r1) = st[2], st[3]
        r0.wait_recv()
        r1.wait_recv()
        fa = step(p, 2)
        v = blk(fa, q, 0, half)
        second.append(
            (fa, sender.start(v, v, dev(p, step(q, 1))), sender.start(v, v, dev(p, step(q, 3))))
        )
    yield
    last = []
    for i in range(4):
        for (p, q, dev, blk, own), st in zip(flows, state):
            pa, c, d = st[2][i]
            c.wait_recv()
            v = blk(pa, step(q, 3), 0, quarter)
            last.append(sender.start(v, v, dev(p, step(q, 1))))
            d.wait_recv()
            v = blk(pa, step(q, 1), quarter, quarter)
            last.append(sender.start(v, v, dev(p, step(q, 3))))
    yield
    for copy in last:
        copy.wait_recv()


def entry_kernel(
    tok_ref,
    qkv_ref,
    meta_ref,
    tok_out,
    qkv_out,
    meta_out,
    tok_send,
    tok_recv,
    qkv_send,
    qkv_recv,
    meta_send,
    meta_recv,
    own_sem,
):
    row = lax.axis_index("row")
    col = lax.axis_index("col")
    x, y = col // 4, col % 4
    peers = [(row, (col + i) % 16) for i in range(1, 16)]
    own = [
        pltpu.make_async_copy(tok_ref, tok_out.at[col], own_sem.at[0]),
        pltpu.make_async_copy(qkv_ref, qkv_out.at[col], own_sem.at[1]),
        pltpu.make_async_copy(meta_ref, meta_out.at[col], own_sem.at[2]),
    ]
    for copy in own:
        copy.start()
    greet(peers)
    tok_sender = Sender(tok_send, tok_recv)
    qkv_sender = Sender(qkv_send, qkv_recv)
    meta_sender = Sender(meta_send, meta_recv)
    runs = [
        torus_gather(tok_ref, tok_out, row, x, y, tok_sender),
        torus_gather(qkv_ref, qkv_out, row, x, y, qkv_sender),
    ]
    for run in runs:
        next(run)
    for peer in peers:
        meta_sender.start(meta_ref, meta_out.at[col], peer)
    for _ in range(3):
        for run in runs:
            next(run)
    for run in runs:
        next(run, None)
    for copy in meta_sender.copies:
        copy.wait_recv()
    for sender in (tok_sender, qkv_sender, meta_sender):
        for copy in sender.copies:
            copy.wait_send()
    for copy in own:
        copy.wait()


def entry_gather(tok, qkv, meta):
    arrays = (tok, qkv, meta)
    return pl.pallas_call(
        entry_kernel,
        out_shape=[jax.ShapeDtypeStruct((16,) + a.shape, a.dtype) for a in arrays],
        in_specs=[HBM] * 3,
        out_specs=[HBM] * 3,
        scratch_shapes=[pltpu.SemaphoreType.DMA((40,))] * 4
        + [pltpu.SemaphoreType.DMA((15,))] * 2
        + [pltpu.SemaphoreType.DMA((3,))],
        compiler_params=pltpu.CompilerParams(collective_id=0, has_side_effects=True),
        name="entry_gather",
    )(tok, qkv, meta)


def home_kernel(in_ref, out_ref, send_sem, recv_sem, own_sem):
    row = lax.axis_index("row")
    col = lax.axis_index("col")
    peers = [(col + i) % 16 for i in range(1, 16)]
    own = pltpu.make_async_copy(in_ref.at[col], out_ref.at[col], own_sem)
    own.start()
    greet([(row, c) for c in peers])
    sender = Sender(send_sem, recv_sem)
    for c in peers:
        sender.start(in_ref.at[c], out_ref.at[col], (row, c))
    own.wait()
    for copy in sender.copies:
        copy.wait()


def send_home(packed):
    return pl.pallas_call(
        home_kernel,
        out_shape=jax.ShapeDtypeStruct(packed.shape, packed.dtype),
        in_specs=[HBM],
        out_specs=HBM,
        scratch_shapes=[
            pltpu.SemaphoreType.DMA((15,)),
            pltpu.SemaphoreType.DMA((15,)),
            pltpu.SemaphoreType.DMA,
        ],
        compiler_params=pltpu.CompilerParams(collective_id=1, has_side_effects=True),
        name="send_home",
    )(packed)


def scatter_kernel(
    part_ref, u_in, out_ref, u_ref, send_sem, recv_sem, u_send, u_recv, own_sem, mine, theirs
):
    row, col, z, core = row_place()
    tokens = mine.shape[1]
    half = tokens // 2
    loads = [
        pltpu.make_async_copy(part_ref.at[zz, core], mine.at[zz], own_sem.at[zz])
        for zz in range(4)
    ]
    for copy in loads:
        copy.start()
    greet(row_neighbours(col, z, core))
    sender = Sender(send_sem, recv_sem)
    partner = (z * 2 + 1 - core, col)
    order = [(z + 2) % 4, (z + 1) % 4, (z + 3) % 4, z]
    swaps = [
        sender.start(part_ref.at[zz, 1 - core], theirs.at[i], partner)
        for i, zz in enumerate(order)
    ]
    for copy in loads:
        copy.wait()
    up, down = ((z + 1) % 4) * 2 + core, ((z + 3) % 4) * 2 + core
    sent = []
    relayed = []
    for i, zz in enumerate(order):
        swaps[i].wait_recv()
        theirs[i] = (theirs[i].astype(f32) + mine[zz].astype(f32)).astype(bf16)
        if i == 0:
            top, bottom = pl.ds(0, half), pl.ds(half, half)
            relayed.append(sender.start(theirs.at[0, top], out_ref.at[4, top], (up, col)))
            relayed.append(sender.start(theirs.at[0, bottom], out_ref.at[4, bottom], (down, col)))
        elif i == 1:
            sent.append(sender.start(theirs.at[1], out_ref.at[1], (up, col)))
        elif i == 2:
            sent.append(sender.start(theirs.at[2], out_ref.at[2], (down, col)))
    u_sender = Sender(u_send, u_recv)
    keep = pltpu.make_async_copy(theirs.at[3], out_ref.at[3], own_sem.at[4])
    keep.start()
    relayed[0].wait_recv()
    sent.append(sender.start(out_ref.at[4, top], out_ref.at[0, top], (up, col)))
    relayed[1].wait_recv()
    sent.append(sender.start(out_ref.at[4, bottom], out_ref.at[0, bottom], (down, col)))
    ring_gather(u_ref, row, col, z, core, u_sender)
    for copy in sent:
        copy.wait_recv()
    for copy in sender.copies + u_sender.copies:
        copy.wait_send()
    keep.wait()


def row_scatter(part, u, cid):
    tokens = part.shape[2]
    out, u = pl.pallas_call(
        scatter_kernel,
        out_shape=[
            jax.ShapeDtypeStruct((5, tokens, 256), bf16),
            jax.ShapeDtypeStruct(u.shape, u.dtype),
        ],
        in_specs=[HBM] * 2,
        out_specs=[HBM] * 2,
        scratch_shapes=[
            pltpu.SemaphoreType.DMA((10,)),
            pltpu.SemaphoreType.DMA((10,)),
            pltpu.SemaphoreType.DMA((13,)),
            pltpu.SemaphoreType.DMA((13,)),
            pltpu.SemaphoreType.DMA((5,)),
            pltpu.VMEM((4, tokens, 256), bf16),
            pltpu.VMEM((4, tokens, 256), bf16),
        ],
        input_output_aliases={1: 1},
        compiler_params=pltpu.CompilerParams(collective_id=cid, has_side_effects=True),
        name="row_scatter",
    )(part, u)
    return out, u


def pieces(block, specs_of):
    return [pl.BlockSpec(block, functools.partial(specs_of, i)) for i in range(GRP)]


def by_slot(shape):
    rank = len(shape)

    def index(i, g, req, loc, length, row):
        return (loc[g * GRP + i],) + (0,) * rank

    return pieces((1,) + shape, index)


def by_group(shape):
    rank = len(shape)
    return pl.BlockSpec(shape, lambda g, req, loc, length, row: (0, g) + (0,) * (rank - 2))


def own_group(shape):
    return pl.BlockSpec(shape, lambda g, req, loc, length, row: (row[0], g, 0))


def rows_group(rows, width):
    return pl.BlockSpec((rows, width), lambda g, req, loc, length, row: (g, 0))


def whole(shape):
    rank = len(shape)
    return pl.BlockSpec(
        shape, lambda g, req, loc, length, row: (0,) * rank, pipeline_mode=pl.Buffered(1)
    )


def staged(kernel, name, table, in_specs, out_specs, out_shape, args):
    return pl.pallas_call(
        kernel,
        out_shape=out_shape,
        grid_spec=pltpu.PrefetchScalarGridSpec(
            num_scalar_prefetch=4,
            grid=(K // GRP,),
            in_specs=in_specs,
            out_specs=out_specs,
        ),
        compiler_params=pltpu.CompilerParams(vmem_limit_bytes=60 << 20),
        name=name,
    )(*table, *args)


def slot_rows(i):
    return slice(i * SLOT, (i + 1) * SLOT)


def rank_sum(buf, first):
    total = buf[0, first : first + RANK, :].astype(f32)
    for r in range(1, 8):
        total = total + buf[r, first : first + RANK, :].astype(f32)
    return total.astype(bf16)


def pack_kernel(req, loc, length, row, *refs):
    toks, shrinks, out = refs[:GRP], refs[GRP : 2 * GRP], refs[2 * GRP]
    for i in range(GRP):
        x = toks[i][0]
        out[0, slot_rows(i), :] = x
        u = dot_nt(x, shrinks[i][0]).astype(bf16)
        for j in range(3):
            out[0, TOK + j * RANK : TOK + (j + 1) * RANK, slot_rows(i)] = u[
                :, j * RANK : (j + 1) * RANK
            ]


def attend_kernel(req, loc, length, row, *refs):
    buf, weight = refs[0], refs[1]
    expands, shrinks, out = refs[2 : 2 + GRP], refs[2 + GRP : 2 + 2 * GRP], refs[-1]
    base = dot(buf[0, :TOK, :], weight[0:256, :])
    for r in range(1, 8):
        base = base + dot(buf[r, :TOK, :], weight[r * 256 : (r + 1) * 256, :])
    reduced = [rank_sum(buf, TOK + j * RANK) for j in range(3)]
    g = pl.program_id(0)
    lane = lax.broadcasted_iota(jnp.int32, (SLOT, SLOT), 1)
    for i in range(GRP):
        deltas = [
            dot(reduced[j][:, slot_rows(i)], expands[i][0, j]).astype(bf16).astype(f32)
            for j in range(3)
        ]
        valid = lane < length[g * GRP + i]
        contexts = []
        for h in range(2):
            q, k, v = [
                (
                    base[slot_rows(i), h * 384 + j * HD : h * 384 + (j + 1) * HD]
                    + lowrank_scale * deltas[j][:, h * HD : (h + 1) * HD]
                ).astype(bf16)
                for j in range(3)
            ]
            scores = dot_nt(q, k) / math.sqrt(HD)
            weights = jnp.where(valid, jnp.exp(scores), 0.0)
            probs = (weights / jnp.sum(weights, axis=1, keepdims=True)).astype(bf16)
            contexts.append(dot(probs, v).astype(bf16))
        context = jnp.concatenate(contexts, axis=1)
        out[0, slot_rows(i), :] = context
        out[0, TOK:, slot_rows(i)] = dot_nt(context, shrinks[i][0]).astype(bf16)


def stats_of(values):
    lane = lax.broadcasted_iota(jnp.int32, (TOK, 128), 1)
    one = jnp.sum(values, axis=1, keepdims=True)
    two = jnp.sum(values * values, axis=1, keepdims=True)
    flipped = jnp.where(lane < 64, one, two).T
    return jnp.concatenate([flipped[0:8], flipped[64:72]], axis=0)


def norm_of(values, stats, gain, shift):
    total = stats[0]
    for r in range(1, 8):
        total = total + stats[r]
    total = total * (1.0 / D)
    mean = total[0:1, :]
    square = total[8:9, :]
    factor = lax.rsqrt(square - mean * mean + eps)
    both = jnp.concatenate(
        [jnp.broadcast_to(mean, (8, TOK)), jnp.broadcast_to(factor, (8, TOK))] + [jnp.zeros((112, TOK), f32)],
        axis=0,
    ).T
    return (values - both[:, 0:1]) * both[:, 8:9] * gain + shift


def mix_kernel(req, loc, length, row, *refs):
    buf, tok, weight = refs[:3]
    expands, out, stats = refs[3 : 3 + GRP], refs[-2], refs[-1]
    base = dot(buf[0, :TOK, :], weight[0:256, :])
    for r in range(1, 8):
        base = base + dot(buf[r, :TOK, :], weight[r * 256 : (r + 1) * 256, :])
    reduced = rank_sum(buf, TOK)
    for i in range(GRP):
        delta = dot(reduced[:, slot_rows(i)], expands[i][0]).astype(bf16).astype(f32)
        out[slot_rows(i), :] = (
            tok[0, slot_rows(i), :].astype(f32) + base[slot_rows(i), :] + lowrank_scale * delta
        )
    stats[...] = stats_of(out[...])


def first_kernel(req, loc, length, row, *refs):
    pre, stats, gain, shift = refs[:4]
    shrinks, out = refs[4 : 4 + GRP], refs[-1]
    first = norm_of(pre[...], stats, gain[...], shift[...]).astype(bf16)
    out[0, :TOK, :] = first
    for i in range(GRP):
        out[0, TOK:, slot_rows(i)] = dot_nt(first[slot_rows(i), :], shrinks[i][0]).astype(bf16)


def gelu(v):
    return 0.5 * v * (1.0 + jnp.tanh(math.sqrt(2.0 / math.pi) * (v + 0.044715 * (v * v * v))))


def hidden_kernel(req, loc, length, row, *refs):
    buf, widen, contract = refs[:3]
    expands, shrinks = refs[3 : 3 + GRP], refs[3 + GRP : 3 + 2 * GRP]
    part, ud = refs[-2], refs[-1]
    base = dot(buf[0, :TOK, :], widen[0:256, :])
    for r in range(1, 8):
        base = base + dot(buf[r, :TOK, :], widen[r * 256 : (r + 1) * 256, :])
    reduced = rank_sum(buf, TOK)
    rows = []
    for i in range(GRP):
        delta = dot(reduced[:, slot_rows(i)], expands[i][0]).astype(bf16).astype(f32)
        hidden = gelu(base[slot_rows(i), :] + lowrank_scale * delta).astype(bf16)
        rows.append(hidden)
        ud[0, :, slot_rows(i)] = dot_nt(hidden, shrinks[i][0]).astype(bf16)
    hidden = jnp.concatenate(rows, axis=0)
    for r in range(8):
        part[r // 2, r % 2] = dot_nt(hidden, contract[r * 256 : (r + 1) * 256, :]).astype(bf16)


def second_kernel(req, loc, length, row, *refs):
    summed, ud, first = refs[:3]
    expands, out, stats = refs[3 : 3 + GRP], refs[-2], refs[-1]
    reduced = rank_sum(ud, 0)
    base = summed[0].astype(f32)
    for r in range(1, 4):
        base = base + summed[r].astype(f32)
    for i in range(GRP):
        delta = dot(reduced[:, slot_rows(i)], expands[i][0]).astype(bf16).astype(f32)
        out[slot_rows(i), :] = (
            first[0, slot_rows(i), :].astype(f32) + base[slot_rows(i), :] + lowrank_scale * delta
        )
    stats[...] = stats_of(out[...])


def last_kernel(req, loc, length, row, pre, stats, gain, shift, out):
    out[...] = norm_of(pre[...], stats, gain[...], shift[...]).astype(bf16)


def shards(
    tokens,
    lengths,
    adapter_ids,
    adapter_place,
    attention_qkv_weight,
    attention_out_weight,
    widen_weight,
    contract_weight,
    first_gain,
    first_shift,
    second_gain,
    second_shift,
    attend_shrink,
    attend_expand,
    output_shrink,
    output_expand,
    upward_shrink,
    upward_expand,
    downward_shrink,
    downward_expand,
):
    i32 = jnp.int32
    col = lax.axis_index("col")
    row = lax.axis_index("row")
    stored = attend_shrink.shape[0]
    match = adapter_ids[:, None] == jnp.arange(adapter_place.shape[0], dtype=i32)[None, :]
    position = jnp.sum(jnp.where(match, adapter_place[None, :], 0), axis=1)
    meta = jnp.zeros((8, 128), i32)
    meta = meta.at[0, :REQ_COL].set(position).at[1, :REQ_COL].set(lengths)
    tok_all, qkv_all, meta_all = entry_gather(tokens.T, attention_qkv_weight, meta)
    out_all = lax.all_gather(attention_out_weight, "col", axis=0, tiled=True)
    widen_all = lax.all_gather(widen_weight, "col", axis=0, tiled=True)
    contract_all = lax.all_gather(contract_weight, "col", axis=0, tiled=True)
    qkv_all = qkv_all.reshape(D, -1)
    tok_all = tok_all.reshape(64, SLOT, 256)

    requests = 64
    position = meta_all[:, 0, :REQ_COL].reshape(requests)
    length = meta_all[:, 1, :REQ_COL].reshape(requests)
    owner, local = position // stored, position % stored
    n = jnp.arange(requests, dtype=i32)
    same = (owner[None, :] == owner[:, None]) & (n[None, :] < n[:, None])
    rank = jnp.sum(same.astype(i32), axis=1)
    near = jnp.sum((same & (n[None, :] // REQ_COL == n[:, None] // REQ_COL)).astype(i32), axis=1)
    waves = (jnp.max(rank) + K) // K
    most = -(-32 // K)
    slots = jnp.arange(most * K, dtype=i32)
    mine = owner == col
    hit = mine[None, :] & (rank[None, :] == slots[:, None])
    req = jnp.sum(jnp.where(hit, n[None, :], 0), axis=1)
    loc = jnp.sum(jnp.where(hit, local[None, :], 0), axis=1)
    lens = jnp.maximum(jnp.sum(jnp.where(hit, length[None, :], 0), axis=1), 1)
    pair = jnp.arange(32, dtype=i32)
    out_hit = mine[None, :] & ((n // REQ_COL * 2 + near)[None, :] == pair[:, None])
    out_slot = jnp.sum(jnp.where(out_hit, rank[None, :], 0), axis=1)
    home_n = col * REQ_COL + jnp.arange(REQ_COL, dtype=i32)
    home_hit = home_n[:, None] == n[None, :]
    home_from = jnp.sum(jnp.where(home_hit, (owner * 2 + near)[None, :], 0), axis=1)
    row_id = row.astype(i32)[None]
    groups = K // GRP
    tall = K * SLOT
    gain1 = first_gain[None, :]
    shift1 = lax.dynamic_slice_in_dim(first_shift, row * 256, 256, 0)[None, :]
    gain2 = lax.dynamic_slice_in_dim(second_gain, row * 256, 256, 0)[None, :]
    shift2 = lax.dynamic_slice_in_dim(second_shift, row * 256, 256, 0)[None, :]

    def wave(w):
        table = tuple(
            lax.dynamic_slice_in_dim(t, w * K, K, 0) for t in (req, loc, lens)
        ) + (row_id,)

        def shape(*dims, dtype=bf16):
            return jax.ShapeDtypeStruct(dims, dtype)

        def token_slot(i, g, req, loc, length, row):
            return (req[g * GRP + i], 0, 0)

        high = TOK + 3 * RANK
        low = TOK + RANK
        buf1 = staged(
            pack_kernel,
            "pack",
            table,
            pieces((1, SLOT, 256), token_slot) + by_slot((3 * RANK, 256)),
            own_group((1, high, 256)),
            shape(8, groups * high, 256),
            [tok_all] * GRP + [attend_shrink] * GRP,
        )
        buf1 = row_gather(buf1, 2)
        buf2 = staged(
            attend_kernel,
            "attend",
            table,
            [by_group((8, high, 256)), whole((D, 768))]
            + by_slot((3, RANK, 256))
            + by_slot((RANK, 256)),
            own_group((1, low, 256)),
            shape(8, groups * low, 256),
            [buf1, qkv_all] + [attend_expand] * GRP + [output_shrink] * GRP,
        )
        buf2 = row_gather(buf2, 3)
        pre, stats = staged(
            mix_kernel,
            "mix",
            table,
            [by_group((8, low, 256)), own_group((1, high, 256)), whole((D, 256))]
            + by_slot((RANK, 256)),
            [rows_group(TOK, 256), rows_group(16, 256)],
            [shape(tall, 256, dtype=f32), shape(groups * 16, 256, dtype=f32)],
            [buf2, buf1, out_all] + [output_expand] * GRP,
        )
        stats = stat_gather(stats, 4)
        buf3 = staged(
            first_kernel,
            "first",
            table,
            [rows_group(TOK, 256), by_group((8, 16, 256)), whole((1, 256)), whole((1, 256))]
            + by_slot((RANK, 256)),
            own_group((1, low, 256)),
            shape(8, groups * low, 256),
            [pre, stats, gain1, shift1] + [upward_shrink] * GRP,
        )
        buf3 = row_gather(buf3, 3)
        part, ud = staged(
            hidden_kernel,
            "hidden",
            table,
            [by_group((8, low, 256)), whole((D, 1024)), whole((D, 1024))]
            + by_slot((RANK, 1024))
            + by_slot((RANK, 1024)),
            [
                pl.BlockSpec((4, 2, TOK, 256), lambda g, req, loc, length, row: (0, 0, g, 0)),
                own_group((1, RANK, 256)),
            ],
            [shape(4, 2, tall, 256), shape(8, groups * RANK, 256)],
            [buf3, widen_all, contract_all]
            + [upward_expand] * GRP
            + [downward_shrink] * GRP,
        )
        summed, ud = row_scatter(part, ud, 5)
        pre, stats = staged(
            second_kernel,
            "second",
            table,
            [by_group((4, TOK, 256)), by_group((8, RANK, 256)), own_group((1, low, 256))]
            + by_slot((RANK, 256)),
            [rows_group(TOK, 256), rows_group(16, 256)],
            [shape(tall, 256, dtype=f32), shape(groups * 16, 256, dtype=f32)],
            [summed, ud, buf3] + [downward_expand] * GRP,
        )
        stats = stat_gather(stats, 4)
        return staged(
            last_kernel,
            "last",
            table,
            [rows_group(TOK, 256), by_group((8, 16, 256)), whole((1, 256)), whole((1, 256))],
            rows_group(TOK, 256),
            shape(tall, 256),
            [pre, stats, gain2, shift2],
        )

    result = wave(0)

    def quick(result):
        return jnp.take(result.reshape(K, SLOT, 256), jnp.minimum(out_slot, K - 1), axis=0)

    def longer(result):
        held = jnp.zeros((most, tall, 256), bf16)
        held = lax.dynamic_update_index_in_dim(held, result, 0, 0)
        held = lax.fori_loop(
            1, waves, lambda w, h: lax.dynamic_update_index_in_dim(h, wave(w), w, 0), held
        )
        return jnp.take(held.reshape(most * K, SLOT, 256), out_slot, axis=0)

    packed = lax.cond(waves > 1, longer, quick, result)
    arrived = send_home(packed.reshape(16, 2 * SLOT, 256))
    own = jnp.take(arrived.reshape(32, SLOT, 256), home_from, axis=0).reshape(TOK, 256)
    wide = lax.all_gather(own.T, "row", axis=0, tiled=True)
    return wide


def solution(mesh):
    return jax.shard_map(
        shards,
        mesh=mesh,
        in_specs=(
            P("row", "col"),
            P("col"),
            P("col"),
            P(),
            P("col", "row"),
            P("col", "row"),
            P("col", "row"),
            P("col", "row"),
            P("row"),
            P(),
            P(),
            P(),
            P("col", None, "row"),
            P("col", None, None, "row"),
            P("col", None, "row"),
            P("col", None, "row"),
            P("col", None, "row"),
            P("col", None, "row"),
            P("col", None, "row"),
            P("col", None, "row"),
        ),
        out_specs=P(None, "col"),
        check_vma=False,
    )
```

time: 926 us -> 299 us (0.32); the launches traced: 915 us -> 298 us
  waiting for transfers between devices: 691 us -> 29.1 us
  Pallas kernels: 0 us -> 236 us
  matrix products: 60.5 us -> 0 us
  local copies, waits for them, and re-layouts: 71.5 us -> 12.1 us
  starting transfers between devices: 56.7 us -> 0.12 us
  blocking collectives: 12.2 us -> 0 us
    psum x5 -> x0, waiting for transfers between devices: 298 us -> none  [row_total(): return lax.psum(value.astype(jnp.bfloat16), 'row').astype(jnp.float32)]
    pallas_call x0 -> x15, Pallas kernels: none -> 236 us  [the longest x3 78.1 us: row_gather(): pl.pallas_call(row_gather_kernel, out_shape=jax.ShapeDtypeStruct(buf.shap...]
    all_to_all x9 -> x0, waiting for transfers between devices: 202 us -> none  [the longest x4 109 us: sent_delta(): lax.all_to_all(lowrank_update.reshape(columns, out_width, capacity * slot...]
    all_gather x7 -> x4, waiting for transfers between devices: 187 us -> 27 us  [the longest x1 26.9 us: shards(): wide = lax.all_gather(own.T, 'row', axis=0, tiled=True)]
    dot_general x22 -> x0, matrix products: 60.5 us -> none  [the longest x4 15.3 us: apply_slots(): jnp.einsum('ocki,oics->ocks', shrink, arrived, preferred_element_type=jnp...]
    all_to_all x9 -> x0, starting transfers between devices: 55.8 us -> none  [the longest x4 26.9 us: sent_delta(): lax.all_to_all(lowrank_update.reshape(columns, out_width, capacity * slot...]
    convert_element_type x9 -> x0, local copies, waits for them, and re-layouts: 36.1 us -> none  [the longest x3 23.7 us: apply_slots(): return expand_rule(expand, reduced).astype(jnp.bfloat16)]
    gather x8 -> x2, local copies, waits for them, and re-layouts: 18.9 us -> 2.51 us  [the longest x1 1.9 us: shards(): jnp.take(arrived.reshape(32, SLOT, 256), home_from, axis=0)]
  transfers between devices with their start and end apart: 21 -> 4, of which waited for: 19 -> 1; matrix products, arithmetic and copies ran while one was open for 9% -> 3% of each run, Pallas kernels for 0% -> 52%
where the time goes in v1:
time: 299 us; the launch traced here: 298 us
  Pallas kernels  236 us (79%)
  waiting for transfers between devices  29.1 us (10%)
  between operations  14.1 us (5%)
  local copies, waits for them, and re-layouts  12.1 us (4%)
  other arithmetic  6.51 us (2%)
    pallas_call x3, Pallas kernels, row_gather(): pl.pallas_call(row_gather_kernel, out_shape=jax.ShapeDtypeStruct(buf.shap...  78.1 us
    pallas_call x7, Pallas kernels, staged(): pl.pallas_call(kernel, out_shape=out_shape, grid_spec=pltpu.PrefetchScala...  51.9 us
    pallas_call x1, Pallas kernels, entry_gather(): pl.pallas_call(entry_kernel, out_shape=[jax.ShapeDtypeStruct((16,) + a.sh...  39 us
    pallas_call x1, Pallas kernels, row_scatter(): pl.pallas_call(scatter_kernel, out_shape=[jax.ShapeDtypeStruct((5, tokens...  28.2 us
    all_gather x1, waiting for transfers between devices, shards(): wide = lax.all_gather(own.T, 'row', axis=0, tiled=True)  26.9 us
    pallas_call x2, Pallas kernels, stat_gather(): pl.pallas_call(stat_gather_kernel, out_shape=jax.ShapeDtypeStruct((8,) +...  21.4 us
    pallas_call x1, Pallas kernels, send_home(): pl.pallas_call(home_kernel, out_shape=jax.ShapeDtypeStruct(packed.shape,...  17.2 us
  transfers between devices with their start and end apart: 4, of which 1 were waited for; matrix products, arithmetic and copies ran while one was open for 3% of the time, Pallas kernels for 52%

profile of v1, /device:TPU:1, one launch (start us, length us, event | category | flops | bytes accessed | tf_op | source)
XLA Modules:
  0.0 298.0 jit_solution(8898609327584444032)
XLA Ops:
  6.5 0.7 all-gather.5.cloned.1.call-update
  7.3 0.7 all-gather.7.cloned.1.call-update
  8.1 0.7 all-gather.9.cloned.1.call-update
  8.8 1.7 copy.33
  10.5 0.9 select_reduce_fusion.4
  11.3 0.8 scatter.9.meta_ref
  12.7 39.0 %entry_gather.1 = (bf16[16,256,256]{2,1,0:T(8,128)(2,1)S(1)}, bf16[16,128,768]{2,1,0:T(8,128)(2,1)}, s32[16,8,128]{2,1,0:T(8,128)}) custom-call(bf16[256,256]{1,0:T(8,128)(2,1)} %bitcast.42, bf16[128,768]{1,0:T(8,128)(2,1)} %qkv_ref.1, s32[8,128]{1,0:T(8,128)} %copy-done.27), custom_call_target="tpu_custom_call" | custom-call | tf_op jit(solution)/shard_map/entry_gather/pallas_call | solution.py:306
  51.7 1.1 slice_reduce_fusion
  54.7 3.7 %pack.2.in_ref = bf16[8,1344,256]{2,1,0:T(8,128)(2,1)} custom-call(s32[12]{0:T(128)S(1)} %bitcast.58, s32[12]{0:T(128)S(1)} %bitcast.51, s32[12]{0:T(128)S(1)} %bitcast.65, s32[1]{0:T(128)} %bitcast.7.row, bf16[64,64,256]{2,1,0:T(8,128)(2,1)S(1)} %bitcast.29, bf16[64,64,256]{2,1,0:T(8,128)(2,1)S(1)} %bitcast.30, bf16[64,64,256]{2,1,0:T(8,128)(2,1)S(1)} %bitcast.31, ...), custom_call_target="tpu_custom_call" | custom-call | tf_op jit(solution)/shard_map/pack/pallas_call | solution.py:461
  58.4 33.3 %row_gather.6.refs_0_.refs_1_ = bf16[8,1344,256]{2,1,0:T(8,128)(2,1)} custom-call(bf16[8,1344,256]{2,1,0:T(8,128)(2,1)} %pack.2.in_ref), custom_call_target="tpu_custom_call", output_to_operand_aliasing={{}: (0, {})} | custom-call | tf_op jit(solution)/shard_map/row_gather/pallas_call | solution.py:130
  91.8 16.1 %attend.2.in_ref = bf16[8,960,256]{2,1,0:T(8,128)(2,1)} custom-call(s32[12]{0:T(128)S(1)} %bitcast.59, s32[12]{0:T(128)S(1)} %bitcast.52, s32[12]{0:T(128)S(1)} %bitcast.66, s32[1]{0:T(128)} %bitcast.7.row, bf16[8,1344,256]{2,1,0:T(8,128)(2,1)} %row_gather.6.refs_0_.refs_1_, bf16[2048,768]{1,0:T(8,128)(2,1)} %bitcast.34, bf16[16,3,64,256]{3,2,1,0:T(8,128)(2,1)} %refs_5_.7, ...), custom_call_target="tpu_custom_call" | custom-call | tf_op jit(solution)/shard_map/attend/pallas_call | solution.py:461
  107.8 22.4 %row_gather.7.refs_0_ = bf16[8,960,256]{2,1,0:T(8,128)(2,1)} custom-call(bf16[8,960,256]{2,1,0:T(8,128)(2,1)} %attend.2.in_ref), custom_call_target="tpu_custom_call", output_to_operand_aliasing={{}: (0, {})} | custom-call | tf_op jit(solution)/shard_map/row_gather/pallas_call | solution.py:130
  130.2 0.8 dynamic_slice.30
  131.0 0.8 dynamic_slice.31
  131.8 0.8 dynamic_slice.32
  134.2 5.5 %mix.2 = (f32[768,256]{1,0:T(8,128)}, f32[48,256]{1,0:T(8,128)}) custom-call(s32[12]{0:T(128)S(1)} %bitcast.60, s32[12]{0:T(128)S(1)} %bitcast.53, s32[12]{0:T(128)S(1)} %bitcast.67, s32[1]{0:T(128)} %bitcast.7.row, bf16[8,960,256]{2,1,0:T(8,128)(2,1)} %row_gather.7.refs_0_, bf16[8,1344,256]{2,1,0:T(8,128)(2,1)} %row_gather.6.refs_0_.refs_1_, ...), custom_call_target="tpu_custom_call" | custom-call | tf_op jit(solution)/shard_map/mix/pallas_call | solution.py:461
  139.8 9.9 %stat_gather.4.refs_1_ = f32[8,48,256]{2,1,0:T(8,128)} custom-call(f32[48,256]{1,0:T(8,128)} %get-tuple-element.299.in_ref), custom_call_target="tpu_custom_call" | custom-call | tf_op jit(solution)/shard_map/stat_gather/pallas_call | solution.py:158
  149.7 4.1 %first.2.in_ref = bf16[8,960,256]{2,1,0:T(8,128)(2,1)} custom-call(s32[12]{0:T(128)S(1)} %bitcast.61, s32[12]{0:T(128)S(1)} %bitcast.54, s32[12]{0:T(128)S(1)} %bitcast.68, s32[1]{0:T(128)} %bitcast.7.row, f32[768,256]{1,0:T(8,128)} %get-tuple-element.298.refs_0_, f32[8,48,256]{2,1,0:T(8,128)} %stat_gather.4.refs_1_, f32[1,256]{1,0:T(1,128)S(1)} %bitcast.50, ...), custom_call_target="tpu_custom_call" | custom-call | tf_op jit(solution)/shard_map/first/pallas_call | solution.py:461
  153.8 22.4 %row_gather.8.refs_0_.refs_2_ = bf16[8,960,256]{2,1,0:T(8,128)(2,1)} custom-call(bf16[8,960,256]{2,1,0:T(8,128)(2,1)} %first.2.in_ref), custom_call_target="tpu_custom_call", output_to_operand_aliasing={{}: (0, {})} | custom-call | tf_op jit(solution)/shard_map/row_gather/pallas_call | solution.py:130
  176.3 15.1 %hidden.2 = (bf16[4,2,768,256]{3,2,1,0:T(8,128)(2,1)}, bf16[8,192,256]{2,1,0:T(8,128)(2,1)}) custom-call(s32[12]{0:T(128)S(1)} %bitcast.62, s32[12]{0:T(128)S(1)} %bitcast.55, s32[12]{0:T(128)S(1)} %bitcast.69, s32[1]{0:T(128)} %bitcast.7.row, bf16[8,960,256]{2,1,0:T(8,128)(2,1)} %row_gather.8.refs_0_.refs_2_, ...), custom_call_target="tpu_custom_call" | custom-call | tf_op jit(solution)/shard_map/hidden/pallas_call | solution.py:461
  191.4 28.2 %row_scatter.2 = (bf16[5,768,256]{2,1,0:T(8,128)(2,1)}, bf16[8,192,256]{2,1,0:T(8,128)(2,1)}) custom-call(bf16[4,2,768,256]{3,2,1,0:T(8,128)(2,1)} %get-tuple-element.300.part_ref, bf16[8,192,256]{2,1,0:T(8,128)(2,1)} %get-tuple-element.301.u_in), custom_call_target="tpu_custom_call", output_to_operand_aliasing={{1}: (1, {})} | custom-call | tf_op jit(solution)/shard_map/row_scatter/pallas_call | solution.py:403
  219.6 4.3 %second.2 = (f32[768,256]{1,0:T(8,128)}, f32[48,256]{1,0:T(8,128)}) custom-call(s32[12]{0:T(128)S(1)} %bitcast.63, s32[12]{0:T(128)S(1)} %bitcast.56, s32[12]{0:T(128)S(1)} %bitcast.70, s32[1]{0:T(128)} %bitcast.7.row, bf16[5,768,256]{2,1,0:T(8,128)(2,1)} %get-tuple-element.302.refs_0_, bf16[8,192,256]{2,1,0:T(8,128)(2,1)} %get-tuple-element.303.refs_1_, ...), custom_call_target="tpu_custom_call" | custom-call | tf_op jit(solution)/shard_map/second/pallas_call | solution.py:461
  223.9 11.5 %stat_gather.5.stats = f32[8,48,256]{2,1,0:T(8,128)} custom-call(f32[48,256]{1,0:T(8,128)} %get-tuple-element.305.in_ref), custom_call_target="tpu_custom_call" | custom-call | tf_op jit(solution)/shard_map/stat_gather/pallas_call | solution.py:158
  235.5 3.0 %last.2 = bf16[768,256]{1,0:T(8,128)(2,1)S(1)} custom-call(s32[12]{0:T(128)S(1)} %bitcast.64, s32[12]{0:T(128)S(1)} %bitcast.57, s32[12]{0:T(128)S(1)} %bitcast.71, s32[1]{0:T(128)} %bitcast.7.row, f32[768,256]{1,0:T(8,128)} %get-tuple-element.304.pre, f32[8,48,256]{2,1,0:T(8,128)} %stat_gather.5.stats, f32[1,256]{1,0:T(1,128)S(1)} %bitcast.45, ...), custom_call_target="tpu_custom_call" | custom-call | tf_op jit(solution)/shard_map/last/pallas_call | solution.py:461
  238.5 2.1 conditional.1
  240.6 0.7 compare_and_fusion
  241.2 1.1 broadcast_select_fusion
  242.4 17.2 %send_home.1 = bf16[16,128,256]{2,1,0:T(8,128)(2,1)} custom-call(bf16[16,128,256]{2,1,0:T(8,128)(2,1)} %bitcast.39), custom_call_target="tpu_custom_call" | custom-call | tf_op jit(solution)/shard_map/send_home/pallas_call | solution.py:335
  259.6 1.9 gather_fusion.2
  261.5 0.8 bitcast_select_fusion
  262.3 26.9 %all-gather.11.cloned.1.call-done = bf16[2048,256]{0,1:T(8,128)(2,1)} async-done(((bf16[256,256]{0,1:T(8,128)(2,1)}), bf16[2048,256]{0,1:T(8,128)(2,1)}) %all-gather.11.cloned.1.call-update) | async-done | bytes 1048592 | tf_op jit(solution)/shard_map/all_gather | solution.py:798
  289.2 2.3 copy.34
  (62 shorter events, 5.4 us)
Async XLA Ops:
  6.5 127.7 %all-gather.5.cloned.1.call-start = ((), (), s32[]{:S(2)}) async-start(), calls=%async_computation | async-start | bytes 1114112 | tf_op jit(solution)/shard_map/all_gather | solution.py:651
  7.3 169.0 %all-gather.7.cloned.1.call-start = ((), (), s32[]{:S(2)}) async-start(), calls=%async_computation.1 | async-start | bytes 4456448 | tf_op jit(solution)/shard_map/all_gather | solution.py:652
  8.0 168.2 %all-gather.9.cloned.1.call-start = ((), (), s32[]{:S(2)}) async-start(), calls=%async_computation.2 | async-start | bytes 4456448 | tf_op jit(solution)/shard_map/all_gather | solution.py:653
  8.7 280.4 %all-gather.11.cloned.1.call-start = ((), (), s32[]{:S(2)}) async-start(), calls=%async_computation.3 | async-start | bytes 1179648 | tf_op jit(solution)/shard_map/all_gather | solution.py:798
  12.1 0.6 copy-start.27
  51.7 6.7 %copy-start.2 = (bf16[16,256,256]{2,1,0:T(8,128)(2,1)}, bf16[16,256,256]{2,1,0:T(8,128)(2,1)S(1)}, u32[]{:S(2)}) copy-start(bf16[16,256,256]{2,1,0:T(8,128)(2,1)S(1)} %get-tuple-element.296) | copy-start | bytes 6291460
  54.7 180.8 %copy-start.24 = (s32[36]{0:T(128)}, s32[36]{0:T(128)S(1)}, u32[]{:S(2)}) copy-start(s32[36]{0:T(128)S(1)} %get-tuple-element.313) | copy-start | bytes 436
  54.7 180.8 %copy-start.25 = (s32[36]{0:T(128)}, s32[36]{0:T(128)S(1)}, u32[]{:S(2)}) copy-start(s32[36]{0:T(128)S(1)} %get-tuple-element.314) | copy-start | bytes 436
  54.7 180.8 %copy-start.26 = (s32[36]{0:T(128)}, s32[36]{0:T(128)S(1)}, u32[]{:S(2)}) copy-start(s32[36]{0:T(128)S(1)} %broadcast_maximum_fusion) | copy-start | bytes 436
  58.4 33.4 %copy-start.4 = (bf16[16,64,256]{2,1,0:T(8,128)(2,1)S(1)}, bf16[16,64,256]{2,1,0:T(8,128)(2,1)}, u32[]{:S(2)}) copy-start(bf16[16,64,256]{2,1,0:T(8,128)(2,1)} %refs_9_.2) | copy-start | bytes 1572868
  107.8 26.4 %copy-start.10 = (bf16[16,64,256]{2,1,0:T(8,128)(2,1)S(1)}, bf16[16,64,256]{2,1,0:T(8,128)(2,1)}, u32[]{:S(2)}) copy-start(bf16[16,64,256]{2,1,0:T(8,128)(2,1)} %refs_6_.8) | copy-start | bytes 1572868
  131.0 18.7 %copy-start.16 = (f32[256]{0:T(256)}, f32[256]{0:T(256)S(1)}, u32[]{:S(2)}) copy-start(f32[256]{0:T(256)S(1)} %dynamic_slice.30) | copy-start | bytes 3076
  131.8 103.7 %copy-start.18 = (f32[256]{0:T(256)}, f32[256]{0:T(256)S(1)}, u32[]{:S(2)}) copy-start(f32[256]{0:T(256)S(1)} %dynamic_slice.31) | copy-start | bytes 3076
  132.5 102.9 %copy-start.20 = (f32[256]{0:T(256)}, f32[256]{0:T(256)S(1)}, u32[]{:S(2)}) copy-start(f32[256]{0:T(256)S(1)} %dynamic_slice.32) | copy-start | bytes 3076
  134.1 15.6 %copy-start.6 = (bf16[16,64,256]{2,1,0:T(8,128)(2,1)S(1)}, bf16[16,64,256]{2,1,0:T(8,128)(2,1)}, u32[]{:S(2)}) copy-start(bf16[16,64,256]{2,1,0:T(8,128)(2,1)} %refs_7_.6) | copy-start | bytes 1572868
  134.2 15.6 %copy-start.22 = (f32[256]{0:T(256)S(1)}, f32[256]{0:T(256)}, u32[]{:S(2)}) copy-start(f32[256]{0:T(256)} %param.36) | copy-start | bytes 3076
  153.8 22.4 %copy-start = (bf16[16,64,1024]{2,1,0:T(8,128)(2,1)S(1)}, bf16[16,64,1024]{2,1,0:T(8,128)(2,1)}, u32[]{:S(2)}) copy-start(bf16[16,64,1024]{2,1,0:T(8,128)(2,1)} %refs_6_.10) | copy-start | bytes 6291460
  191.4 28.2 %copy-start.8 = (bf16[16,64,256]{2,1,0:T(8,128)(2,1)S(1)}, bf16[16,64,256]{2,1,0:T(8,128)(2,1)}, u32[]{:S(2)}) copy-start(bf16[16,64,256]{2,1,0:T(8,128)(2,1)} %refs_6_.11) | copy-start | bytes 1572868
  240.6 20.9 %copy-start.28 = (pred[256]{0:T(512)(128)(4,1)S(1)}, pred[256]{0:T(512)(128)(4,1)}, u32[]{:S(2)}) copy-start(pred[256]{0:T(512)(128)(4,1)} %broadcast_in_dim.151) | copy-start | bytes 772
Sparse Core Ops, SparseCore 0:
  9.5 45.7 all-gather.4
  57.4 51.8 all-gather.6
  111.4 50.8 all-gather.8
  262.4 26.7 all-gather.10

commit v2 on v1

--- a/solution.py
+++ b/solution.py
@@ -91,22 +91,31 @@
     def across(zz, h):
         rest.append(sender.start(part(zz, h), part(zz, h), partner))
 
+    yield
     a0.wait_recv()
     r0 = sender.start(part(down, 0), part(down, 0), dev(up))
     across(down, 0)
     b1.wait_recv()
     r1 = sender.start(part(up, 1), part(up, 1), dev(down))
     across(up, 1)
+    yield
     a1.wait_recv()
     across(down, 1)
     b0.wait_recv()
     across(up, 0)
+    yield
     r0.wait_recv()
     across(far, 0)
     r1.wait_recv()
     across(far, 1)
+    yield
     for copy in rest:
         copy.wait_recv()
+
+
+def finish(run):
+    for _ in run:
+        pass
 
 
 def row_neighbours(col, z, core):
@@ -121,7 +130,7 @@
     row, col, z, core = row_place()
     greet(row_neighbours(col, z, core))
     sender = Sender(send_sem, recv_sem)
-    ring_gather(out_ref, row, col, z, core, sender)
+    finish(ring_gather(out_ref, row, col, z, core, sender))
     for copy in sender.copies:
         copy.wait_send()
 
@@ -249,20 +258,17 @@
         copy.wait_recv()
 
 
+def torus_neighbours(row, x, y):
+    return [
+        (row, (x + 1) % 4 * 4 + y),
+        (row, (x + 3) % 4 * 4 + y),
+        (row, x * 4 + (y + 1) % 4),
+        (row, x * 4 + (y + 3) % 4),
+    ]
+
+
 def entry_kernel(
-    tok_ref,
-    qkv_ref,
-    meta_ref,
-    tok_out,
-    qkv_out,
-    meta_out,
-    tok_send,
-    tok_recv,
-    qkv_send,
-    qkv_recv,
-    meta_send,
-    meta_recv,
-    own_sem,
+    tok_ref, meta_ref, tok_out, meta_out, tok_send, tok_recv, meta_send, meta_recv, own_sem
 ):
     row = lax.axis_index("row")
     col = lax.axis_index("col")
@@ -270,81 +276,127 @@
     peers = [(row, (col + i) % 16) for i in range(1, 16)]
     own = [
         pltpu.make_async_copy(tok_ref, tok_out.at[col], own_sem.at[0]),
-        pltpu.make_async_copy(qkv_ref, qkv_out.at[col], own_sem.at[1]),
-        pltpu.make_async_copy(meta_ref, meta_out.at[col], own_sem.at[2]),
+        pltpu.make_async_copy(meta_ref, meta_out.at[col], own_sem.at[1]),
     ]
     for copy in own:
         copy.start()
     greet(peers)
     tok_sender = Sender(tok_send, tok_recv)
-    qkv_sender = Sender(qkv_send, qkv_recv)
     meta_sender = Sender(meta_send, meta_recv)
-    runs = [
-        torus_gather(tok_ref, tok_out, row, x, y, tok_sender),
-        torus_gather(qkv_ref, qkv_out, row, x, y, qkv_sender),
-    ]
-    for run in runs:
-        next(run)
+    run = torus_gather(tok_ref, tok_out, row, x, y, tok_sender)
+    next(run)
     for peer in peers:
         meta_sender.start(meta_ref, meta_out.at[col], peer)
-    for _ in range(3):
-        for run in runs:
-            next(run)
-    for run in runs:
-        next(run, None)
+    finish(run)
     for copy in meta_sender.copies:
         copy.wait_recv()
-    for sender in (tok_sender, qkv_sender, meta_sender):
+    for sender in (tok_sender, meta_sender):
         for copy in sender.copies:
             copy.wait_send()
     for copy in own:
         copy.wait()
 
 
-def entry_gather(tok, qkv, meta):
-    arrays = (tok, qkv, meta)
+def entry_gather(tok, meta):
+    arrays = (tok, meta)
     return pl.pallas_call(
         entry_kernel,
         out_shape=[jax.ShapeDtypeStruct((16,) + a.shape, a.dtype) for a in arrays],
+        in_specs=[HBM] * 2,
+        out_specs=[HBM] * 2,
+        scratch_shapes=[pltpu.SemaphoreType.DMA((40,))] * 2
+        + [pltpu.SemaphoreType.DMA((15,))] * 2
+        + [pltpu.SemaphoreType.DMA((2,))],
+        compiler_params=pltpu.CompilerParams(collective_id=0, has_side_effects=True),
+        name="entry_gather",
+    )(tok, meta)
+
+
+def wide_gather_kernel(
+    buf_in, qkv_ref, out_ref, buf, qkv_all, out_all,
+    send_sem, recv_sem, q_send, q_recv, o_send, o_recv, own_sem
+):
+    row, col, z, core = row_place()
+    x, y = col // 4, col % 4
+    own = [
+        pltpu.make_async_copy(qkv_ref, qkv_all.at[col], own_sem.at[0]),
+        pltpu.make_async_copy(out_ref, out_all.at[col], own_sem.at[1]),
+    ]
+    for copy in own:
+        copy.start()
+    greet(row_neighbours(col, z, core) + torus_neighbours(row, x, y))
+    senders = [Sender(send_sem, recv_sem), Sender(q_send, q_recv), Sender(o_send, o_recv)]
+    ring = ring_gather(buf, row, col, z, core, senders[0])
+    qkv = torus_gather(qkv_ref, qkv_all, row, x, y, senders[1])
+    out = torus_gather(out_ref, out_all, row, x, y, senders[2])
+    for run in (ring, qkv, qkv, qkv, ring, qkv, out, out, out, out, ring):
+        next(run)
+    for run in (ring, qkv, out):
+        finish(run)
+    for sender in senders:
+        for copy in sender.copies:
+            copy.wait_send()
+    for copy in own:
+        copy.wait()
+
+
+def wide_gather(buf, qkv, out, cid):
+    return pl.pallas_call(
+        wide_gather_kernel,
+        out_shape=[
+            jax.ShapeDtypeStruct(buf.shape, buf.dtype),
+            jax.ShapeDtypeStruct((16,) + qkv.shape, qkv.dtype),
+            jax.ShapeDtypeStruct((16,) + out.shape, out.dtype),
+        ],
         in_specs=[HBM] * 3,
         out_specs=[HBM] * 3,
-        scratch_shapes=[pltpu.SemaphoreType.DMA((40,))] * 4
-        + [pltpu.SemaphoreType.DMA((15,))] * 2
-        + [pltpu.SemaphoreType.DMA((3,))],
-        compiler_params=pltpu.CompilerParams(collective_id=0, has_side_effects=True),
-        name="entry_gather",
-    )(tok, qkv, meta)
-
-
-def home_kernel(in_ref, out_ref, send_sem, recv_sem, own_sem):
-    row = lax.axis_index("row")
-    col = lax.axis_index("col")
+        scratch_shapes=[pltpu.SemaphoreType.DMA((13,))] * 2
+        + [pltpu.SemaphoreType.DMA((40,))] * 4
+        + [pltpu.SemaphoreType.DMA((2,))],
+        input_output_aliases={0: 0},
+        compiler_params=pltpu.CompilerParams(collective_id=cid, has_side_effects=True),
+        name="wide_gather",
+    )(buf, qkv, out)
+
+
+def exit_kernel(pick, in_ref, out_ref, send_sem, recv_sem, r_send, r_recv, own_sem, arrived):
+    row, col, z, core = row_place()
     peers = [(col + i) % 16 for i in range(1, 16)]
-    own = pltpu.make_async_copy(in_ref.at[col], out_ref.at[col], own_sem)
+    here = arrived.at[pl.ds(col * 2, 2)]
+    own = pltpu.make_async_copy(in_ref.at[col], here, own_sem)
     own.start()
-    greet([(row, c) for c in peers])
+    greet([(row, c) for c in peers] + row_neighbours(col, z, core))
     sender = Sender(send_sem, recv_sem)
     for c in peers:
-        sender.start(in_ref.at[c], out_ref.at[col], (row, c))
+        sender.start(in_ref.at[c], here, (row, c))
     own.wait()
     for copy in sender.copies:
-        copy.wait()
-
-
-def send_home(packed):
+        copy.wait_recv()
+    mine = jnp.concatenate([arrived[pick[i]] for i in range(REQ_COL)], axis=0)
+    out_ref[row] = mine.T
+    r_sender = Sender(r_send, r_recv)
+    finish(ring_gather(out_ref, row, col, z, core, r_sender))
+    for copy in sender.copies + r_sender.copies:
+        copy.wait_send()
+
+
+def send_home(packed, pick):
     return pl.pallas_call(
-        home_kernel,
-        out_shape=jax.ShapeDtypeStruct(packed.shape, packed.dtype),
-        in_specs=[HBM],
-        out_specs=HBM,
+        exit_kernel,
+        out_shape=jax.ShapeDtypeStruct((8, 256, TOK), packed.dtype),
+        in_specs=[pl.BlockSpec(memory_space=pltpu.SMEM), HBM],
+        out_specs=pl.BlockSpec(memory_space=pltpu.VMEM),
         scratch_shapes=[
             pltpu.SemaphoreType.DMA((15,)),
             pltpu.SemaphoreType.DMA((15,)),
+            pltpu.SemaphoreType.DMA((13,)),
+            pltpu.SemaphoreType.DMA((13,)),
             pltpu.SemaphoreType.DMA,
+            pltpu.VMEM((32, SLOT, 256), packed.dtype),
         ],
         compiler_params=pltpu.CompilerParams(collective_id=1, has_side_effects=True),
         name="send_home",
-    )(packed)
+    )(pick, packed)
 
 
 def scatter_kernel(
@@ -390,7 +442,7 @@
     sent.append(sender.start(out_ref.at[4, top], out_ref.at[0, top], (up, col)))
     relayed[1].wait_recv()
     sent.append(sender.start(out_ref.at[4, bottom], out_ref.at[0, bottom], (down, col)))
-    ring_gather(u_ref, row, col, z, core, u_sender)
+    finish(ring_gather(u_ref, row, col, z, core, u_sender))
     for copy in sent:
         copy.wait_recv()
     for copy in sender.copies + u_sender.copies:
@@ -647,11 +699,9 @@
     position = jnp.sum(jnp.where(match, adapter_place[None, :], 0), axis=1)
     meta = jnp.zeros((8, 128), i32)
     meta = meta.at[0, :REQ_COL].set(position).at[1, :REQ_COL].set(lengths)
-    tok_all, qkv_all, meta_all = entry_gather(tokens.T, attention_qkv_weight, meta)
-    out_all = lax.all_gather(attention_out_weight, "col", axis=0, tiled=True)
+    tok_all, meta_all = entry_gather(tokens.T, meta)
     widen_all = lax.all_gather(widen_weight, "col", axis=0, tiled=True)
     contract_all = lax.all_gather(contract_weight, "col", axis=0, tiled=True)
-    qkv_all = qkv_all.reshape(D, -1)
     tok_all = tok_all.reshape(64, SLOT, 256)
 
     requests = 64
@@ -684,7 +734,7 @@
     gain2 = lax.dynamic_slice_in_dim(second_gain, row * 256, 256, 0)[None, :]
     shift2 = lax.dynamic_slice_in_dim(second_shift, row * 256, 256, 0)[None, :]
 
-    def wave(w):
+    def wave(w, weights):
         table = tuple(
             lax.dynamic_slice_in_dim(t, w * K, K, 0) for t in (req, loc, lens)
         ) + (row_id,)
@@ -706,7 +756,14 @@
             shape(8, groups * high, 256),
             [tok_all] * GRP + [attend_shrink] * GRP,
         )
-        buf1 = row_gather(buf1, 2)
+        if weights is None:
+            buf1, qkv_all, out_all = wide_gather(
+                buf1, attention_qkv_weight, attention_out_weight, 2
+            )
+            weights = (qkv_all.reshape(D, -1), out_all.reshape(D, -1))
+        else:
+            buf1 = row_gather(buf1, 6)
+        qkv_all, out_all = weights
         buf2 = staged(
             attend_kernel,
             "attend",
@@ -769,7 +826,7 @@
             [summed, ud, buf3] + [downward_expand] * GRP,
         )
         stats = stat_gather(stats, 4)
-        return staged(
+        result = staged(
             last_kernel,
             "last",
             table,
@@ -778,8 +835,9 @@
             shape(tall, 256),
             [pre, stats, gain2, shift2],
         )
-
-    result = wave(0)
+        return result, weights
+
+    result, weights = wave(0, None)
 
     def quick(result):
         return jnp.take(result.reshape(K, SLOT, 256), jnp.minimum(out_slot, K - 1), axis=0)
@@ -788,15 +846,12 @@
         held = jnp.zeros((most, tall, 256), bf16)
         held = lax.dynamic_update_index_in_dim(held, result, 0, 0)
         held = lax.fori_loop(
-            1, waves, lambda w, h: lax.dynamic_update_index_in_dim(h, wave(w), w, 0), held
+            1, waves, lambda w, h: lax.dynamic_update_index_in_dim(h, wave(w, weights)[0], w, 0), held
         )
         return jnp.take(held.reshape(most * K, SLOT, 256), out_slot, axis=0)
 
     packed = lax.cond(waves > 1, longer, quick, result)
-    arrived = send_home(packed.reshape(16, 2 * SLOT, 256))
-    own = jnp.take(arrived.reshape(32, SLOT, 256), home_from, axis=0).reshape(TOK, 256)
-    wide = lax.all_gather(own.T, "row", axis=0, tiled=True)
-    return wide
+    return send_home(packed.reshape(16, 2, SLOT, 256), home_from).reshape(D, TOK)
 
 
 def solution(mesh):

time: 299 us -> 286 us (0.957); the launches traced: 298 us -> 281 us
  waiting for transfers between devices: 29.1 us -> 1.41 us
  Pallas kernels: 236 us -> 253 us
  other arithmetic: 6.51 us -> 2.91 us
    pallas_call x1 -> x2, Pallas kernels: 17.2 us -> 82.5 us  [the longest x1 54.1 us: wide_gather(): pl.pallas_call(wide_gather_kernel, out_shape=[jax.ShapeDtypeStruct(buf.sh...]
    pallas_call x3 -> x2, Pallas kernels: 78.1 us -> 45.6 us  [row_gather(): pl.pallas_call(row_gather_kernel, out_shape=jax.ShapeDtypeStruct(buf.shap...]
    all_gather x2 -> x0, waiting for transfers between devices: 26.9 us -> none  [the longest x1 26.9 us: shards(): wide = lax.all_gather(own.T, 'row', axis=0, tiled=True)]
    pallas_call x1, Pallas kernels: 39 us -> 23.8 us  [entry_gather(): pl.pallas_call(entry_kernel, out_shape=[jax.ShapeDtypeStruct((16,) + a.sh...]
  transfers between devices with their start and end apart: 4 -> 2, of which waited for: 1 -> 0; matrix products, arithmetic and copies ran while one was open for 3% -> 3% of each run, Pallas kernels for 52% -> 58%
where the time goes in v2:
time: 286 us; the launch traced here: 281 us
  Pallas kernels  253 us (88%)
  between operations  14.4 us (5%)
  local copies, waits for them, and re-layouts  9.58 us (3%)
  other arithmetic  2.91 us (1%)
    pallas_call x1, Pallas kernels, wide_gather(): pl.pallas_call(wide_gather_kernel, out_shape=[jax.ShapeDtypeStruct(buf.sh...  54.1 us
    pallas_call x7, Pallas kernels, staged(): pl.pallas_call(kernel, out_shape=out_shape, grid_spec=pltpu.PrefetchScala...  51.4 us
    pallas_call x2, Pallas kernels, row_gather(): pl.pallas_call(row_gather_kernel, out_shape=jax.ShapeDtypeStruct(buf.shap...  45.6 us
    pallas_call x1, Pallas kernels, row_scatter(): pl.pallas_call(scatter_kernel, out_shape=[jax.ShapeDtypeStruct((5, tokens...  28.5 us
    pallas_call x1, Pallas kernels, send_home(): pl.pallas_call(exit_kernel, out_shape=jax.ShapeDtypeStruct((8, 256, TOK),...  28.4 us
    pallas_call x1, Pallas kernels, entry_gather(): pl.pallas_call(entry_kernel, out_shape=[jax.ShapeDtypeStruct((16,) + a.sh...  23.8 us
    pallas_call x2, Pallas kernels, stat_gather(): pl.pallas_call(stat_gather_kernel, out_shape=jax.ShapeDtypeStruct((8,) +...  21.1 us
  transfers between devices with their start and end apart: 2, of which 0 were waited for; matrix products, arithmetic and copies ran while one was open for 3% of the time, Pallas kernels for 58%

profile of v2, /device:TPU:1, one launch (start us, length us, event | category | flops | bytes accessed | tf_op | source)
XLA Modules:
  0.0 281.5 jit_solution(4451041521374618100)
XLA Ops:
  6.5 0.7 all-gather.3.cloned.1.call-update
  7.3 0.7 all-gather.5.cloned.1.call-update
  8.0 1.7 copy.31
  9.7 0.9 select_reduce_fusion.4
  10.5 0.8 scatter.9.meta_ref
  11.3 0.6 copy-done.28
  11.9 23.8 %entry_gather.1 = (bf16[16,256,256]{2,1,0:T(8,128)(2,1)S(1)}, s32[16,8,128]{2,1,0:T(8,128)}) custom-call(bf16[256,256]{1,0:T(8,128)(2,1)} %bitcast.39, s32[8,128]{1,0:T(8,128)} %copy-done.28), custom_call_target="tpu_custom_call" | custom-call | tf_op jit(solution)/shard_map/entry_gather/pallas_call | solution.py:302
  35.8 1.1 slice_reduce_fusion
  37.0 0.2 convert_reduce_fusion
  37.1 0.6 reduce_max.9
  38.8 3.7 %pack.2.buf_in = bf16[8,1344,256]{2,1,0:T(8,128)(2,1)} custom-call(s32[12]{0:T(128)S(1)} %bitcast.55, s32[12]{0:T(128)S(1)} %bitcast.48, s32[12]{0:T(128)S(1)} %bitcast.62, s32[1]{0:T(128)} %bitcast.9.row, bf16[64,64,256]{2,1,0:T(8,128)(2,1)S(1)} %bitcast.24, bf16[64,64,256]{2,1,0:T(8,128)(2,1)S(1)} %bitcast.25, bf16[64,64,256]{2,1,0:T(8,128)(2,1)S(1)} %bitcast.26, ...), custom_call_target="tpu_custom_call" | custom-call | tf_op jit(solution)/shard_map/pack/pallas_call | solution.py:513
  42.4 54.1 %wide_gather.1 = (bf16[8,1344,256]{2,1,0:T(8,128)(2,1)}, bf16[16,128,768]{2,1,0:T(8,128)(2,1)}, bf16[16,128,256]{2,1,0:T(8,128)(2,1)}) custom-call(bf16[8,1344,256]{2,1,0:T(8,128)(2,1)} %pack.2.buf_in, bf16[128,768]{1,0:T(8,128)(2,1)} %qkv_ref.1, bf16[128,256]{1,0:T(8,128)(2,1)} %out_ref.1), custom_call_target="tpu_custom_call", output_to_operand_aliasing={{0}: (0, {})} | custom-call | tf_op jit(solution)/shard_map/wide_gather/pallas_call | solution.py:344
  96.6 16.1 %attend.2.in_ref = bf16[8,960,256]{2,1,0:T(8,128)(2,1)} custom-call(s32[12]{0:T(128)S(1)} %bitcast.56, s32[12]{0:T(128)S(1)} %bitcast.49, s32[12]{0:T(128)S(1)} %bitcast.63, s32[1]{0:T(128)} %bitcast.9.row, bf16[8,1344,256]{2,1,0:T(8,128)(2,1)} %get-tuple-element.257.refs_0_.refs_1_, bf16[2048,768]{1,0:T(8,128)(2,1)} %bitcast.29, ...), custom_call_target="tpu_custom_call" | custom-call | tf_op jit(solution)/shard_map/attend/pallas_call | solution.py:513
  112.7 23.2 %row_gather.5.refs_0_ = bf16[8,960,256]{2,1,0:T(8,128)(2,1)} custom-call(bf16[8,960,256]{2,1,0:T(8,128)(2,1)} %attend.2.in_ref), custom_call_target="tpu_custom_call", output_to_operand_aliasing={{}: (0, {})} | custom-call | tf_op jit(solution)/shard_map/row_gather/pallas_call | solution.py:139
  136.0 5.1 %mix.2 = (f32[768,256]{1,0:T(8,128)}, f32[48,256]{1,0:T(8,128)}) custom-call(s32[12]{0:T(128)S(1)} %bitcast.57, s32[12]{0:T(128)S(1)} %bitcast.50, s32[12]{0:T(128)S(1)} %bitcast.64, s32[1]{0:T(128)} %bitcast.9.row, bf16[8,960,256]{2,1,0:T(8,128)(2,1)} %row_gather.5.refs_0_, bf16[8,1344,256]{2,1,0:T(8,128)(2,1)} %get-tuple-element.257.refs_0_.refs_1_, ...), custom_call_target="tpu_custom_call" | custom-call | tf_op jit(solution)/shard_map/mix/pallas_call | solution.py:513
  141.1 9.9 %stat_gather.4.refs_1_ = f32[8,48,256]{2,1,0:T(8,128)} custom-call(f32[48,256]{1,0:T(8,128)} %get-tuple-element.261.in_ref), custom_call_target="tpu_custom_call" | custom-call | tf_op jit(solution)/shard_map/stat_gather/pallas_call | solution.py:167
  151.0 0.8 dynamic_slice.30
  151.8 4.1 %first.2.in_ref = bf16[8,960,256]{2,1,0:T(8,128)(2,1)} custom-call(s32[12]{0:T(128)S(1)} %bitcast.58, s32[12]{0:T(128)S(1)} %bitcast.51, s32[12]{0:T(128)S(1)} %bitcast.65, s32[1]{0:T(128)} %bitcast.9.row, f32[768,256]{1,0:T(8,128)} %get-tuple-element.260.refs_0_, f32[8,48,256]{2,1,0:T(8,128)} %stat_gather.4.refs_1_, f32[1,256]{1,0:T(1,128)S(1)} %bitcast.47, ...), custom_call_target="tpu_custom_call" | custom-call | tf_op jit(solution)/shard_map/first/pallas_call | solution.py:513
  155.8 22.4 %row_gather.6.refs_0_.refs_2_ = bf16[8,960,256]{2,1,0:T(8,128)(2,1)} custom-call(bf16[8,960,256]{2,1,0:T(8,128)(2,1)} %first.2.in_ref), custom_call_target="tpu_custom_call", output_to_operand_aliasing={{}: (0, {})} | custom-call | tf_op jit(solution)/shard_map/row_gather/pallas_call | solution.py:139
  178.2 0.8 dynamic_slice.31
  179.0 0.8 dynamic_slice.32
  179.9 0.7 select_reduce_fusion.5.pick
  180.6 15.1 %hidden.2 = (bf16[4,2,768,256]{3,2,1,0:T(8,128)(2,1)}, bf16[8,192,256]{2,1,0:T(8,128)(2,1)}) custom-call(s32[12]{0:T(128)S(1)} %bitcast.59, s32[12]{0:T(128)S(1)} %bitcast.52, s32[12]{0:T(128)S(1)} %bitcast.66, s32[1]{0:T(128)} %bitcast.9.row, bf16[8,960,256]{2,1,0:T(8,128)(2,1)} %row_gather.6.refs_0_.refs_2_, ...), custom_call_target="tpu_custom_call" | custom-call | tf_op jit(solution)/shard_map/hidden/pallas_call | solution.py:513
  195.7 28.5 %row_scatter.2 = (bf16[5,768,256]{2,1,0:T(8,128)(2,1)}, bf16[8,192,256]{2,1,0:T(8,128)(2,1)}) custom-call(bf16[4,2,768,256]{3,2,1,0:T(8,128)(2,1)} %get-tuple-element.262.part_ref, bf16[8,192,256]{2,1,0:T(8,128)(2,1)} %get-tuple-element.263.u_in), custom_call_target="tpu_custom_call", output_to_operand_aliasing={{1}: (1, {})} | custom-call | tf_op jit(solution)/shard_map/row_scatter/pallas_call | solution.py:455
  224.2 4.3 %second.2 = (f32[768,256]{1,0:T(8,128)}, f32[48,256]{1,0:T(8,128)}) custom-call(s32[12]{0:T(128)S(1)} %bitcast.60, s32[12]{0:T(128)S(1)} %bitcast.53, s32[12]{0:T(128)S(1)} %bitcast.67, s32[1]{0:T(128)} %bitcast.9.row, bf16[5,768,256]{2,1,0:T(8,128)(2,1)} %get-tuple-element.264.refs_0_, bf16[8,192,256]{2,1,0:T(8,128)(2,1)} %get-tuple-element.265.refs_1_, ...), custom_call_target="tpu_custom_call" | custom-call | tf_op jit(solution)/shard_map/second/pallas_call | solution.py:513
  228.5 11.2 %stat_gather.5.stats = f32[8,48,256]{2,1,0:T(8,128)} custom-call(f32[48,256]{1,0:T(8,128)} %get-tuple-element.267.in_ref), custom_call_target="tpu_custom_call" | custom-call | tf_op jit(solution)/shard_map/stat_gather/pallas_call | solution.py:167
  239.8 3.0 %last.2 = bf16[768,256]{1,0:T(8,128)(2,1)S(1)} custom-call(s32[12]{0:T(128)S(1)} %bitcast.61, s32[12]{0:T(128)S(1)} %bitcast.54, s32[12]{0:T(128)S(1)} %bitcast.68, s32[1]{0:T(128)} %bitcast.9.row, f32[768,256]{1,0:T(8,128)} %get-tuple-element.266.pre, f32[8,48,256]{2,1,0:T(8,128)} %stat_gather.5.stats, f32[1,256]{1,0:T(1,128)S(1)} %bitcast.42, ...), custom_call_target="tpu_custom_call" | custom-call | tf_op jit(solution)/shard_map/last/pallas_call | solution.py:513
  242.8 1.2 conditional.1
  242.8 0.6 gather_fusion
  243.5 0.2 broadcast_select_fusion
  244.0 28.4 %send_home.1 = bf16[8,256,256]{2,1,0:T(8,128)(2,1)} custom-call(s32[4]{0:T(128)} %select_reduce_fusion.5.pick, bf16[16,2,64,256]{3,2,1,0:T(8,128)(2,1)S(1)} %get-tuple-element.578.in_ref), custom_call_target="tpu_custom_call" | custom-call | tf_op jit(solution)/shard_map/send_home/pallas_call | solution.py:384
  272.4 2.3 copy.51
  (47 shorter events, 0.7 us)
Async XLA Ops:
  6.5 174.1 %all-gather.3.cloned.1.call-start = ((), (), s32[]{:S(2)}) async-start(), calls=%async_computation | async-start | bytes 4456448 | tf_op jit(solution)/shard_map/all_gather | solution.py:703
  7.3 173.3 %all-gather.5.cloned.1.call-start = ((), (), s32[]{:S(2)}) async-start(), calls=%async_computation.1 | async-start | bytes 4456448 | tf_op jit(solution)/shard_map/all_gather | solution.py:704
  11.3 0.6 copy-start.28
  35.8 6.6 %copy-start.2 = (bf16[16,256,256]{2,1,0:T(8,128)(2,1)}, bf16[16,256,256]{2,1,0:T(8,128)(2,1)S(1)}, u32[]{:S(2)}) copy-start(bf16[16,256,256]{2,1,0:T(8,128)(2,1)S(1)} %get-tuple-element.256) | copy-start | bytes 6291460
  38.7 201.0 %copy-start.25 = (s32[36]{0:T(128)}, s32[36]{0:T(128)S(1)}, u32[]{:S(2)}) copy-start(s32[36]{0:T(128)S(1)} %get-tuple-element.271) | copy-start | bytes 436
  38.7 201.0 %copy-start.26 = (s32[36]{0:T(128)}, s32[36]{0:T(128)S(1)}, u32[]{:S(2)}) copy-start(s32[36]{0:T(128)S(1)} %get-tuple-element.272) | copy-start | bytes 436
  38.7 201.0 %copy-start.27 = (s32[36]{0:T(128)}, s32[36]{0:T(128)S(1)}, u32[]{:S(2)}) copy-start(s32[36]{0:T(128)S(1)} %broadcast_maximum_fusion) | copy-start | bytes 436
  42.4 54.1 %copy-start.4 = (bf16[16,64,256]{2,1,0:T(8,128)(2,1)S(1)}, bf16[16,64,256]{2,1,0:T(8,128)(2,1)}, u32[]{:S(2)}) copy-start(bf16[16,64,256]{2,1,0:T(8,128)(2,1)} %refs_9_.2) | copy-start | bytes 1572868
  112.7 23.2 %copy-start.10 = (bf16[16,64,256]{2,1,0:T(8,128)(2,1)S(1)}, bf16[16,64,256]{2,1,0:T(8,128)(2,1)}, u32[]{:S(2)}) copy-start(bf16[16,64,256]{2,1,0:T(8,128)(2,1)} %refs_6_.8) | copy-start | bytes 1572868
  112.7 23.2 %copy-start.12 = (bf16[16,128,256]{2,1,0:T(8,128)(2,1)S(1)}, bf16[16,128,256]{2,1,0:T(8,128)(2,1)}, u32[]{:S(2)}) copy-start(bf16[16,128,256]{2,1,0:T(8,128)(2,1)} %get-tuple-element.259) | copy-start | bytes 3145732
  135.9 15.8 %copy-start.6 = (bf16[16,64,256]{2,1,0:T(8,128)(2,1)S(1)}, bf16[16,64,256]{2,1,0:T(8,128)(2,1)}, u32[]{:S(2)}) copy-start(bf16[16,64,256]{2,1,0:T(8,128)(2,1)} %refs_7_.6) | copy-start | bytes 1572868
  135.9 15.8 %copy-start.23 = (f32[256]{0:T(256)S(1)}, f32[256]{0:T(256)}, u32[]{:S(2)}) copy-start(f32[256]{0:T(256)} %param.36) | copy-start | bytes 3076
  151.7 4.1 %copy-start.17 = (f32[256]{0:T(256)}, f32[256]{0:T(256)S(1)}, u32[]{:S(2)}) copy-start(f32[256]{0:T(256)S(1)} %dynamic_slice.30) | copy-start | bytes 3076
  155.8 24.8 %copy-start = (bf16[16,64,1024]{2,1,0:T(8,128)(2,1)S(1)}, bf16[16,64,1024]{2,1,0:T(8,128)(2,1)}, u32[]{:S(2)}) copy-start(bf16[16,64,1024]{2,1,0:T(8,128)(2,1)} %refs_6_.10) | copy-start | bytes 6291460
  179.0 60.8 %copy-start.19 = (f32[256]{0:T(256)}, f32[256]{0:T(256)S(1)}, u32[]{:S(2)}) copy-start(f32[256]{0:T(256)S(1)} %dynamic_slice.31) | copy-start | bytes 3076
  179.7 60.0 %copy-start.21 = (f32[256]{0:T(256)}, f32[256]{0:T(256)S(1)}, u32[]{:S(2)}) copy-start(f32[256]{0:T(256)S(1)} %dynamic_slice.32) | copy-start | bytes 3076
  195.7 28.5 %copy-start.8 = (bf16[16,64,256]{2,1,0:T(8,128)(2,1)S(1)}, bf16[16,64,256]{2,1,0:T(8,128)(2,1)}, u32[]{:S(2)}) copy-start(bf16[16,64,256]{2,1,0:T(8,128)(2,1)} %refs_6_.11) | copy-start | bytes 1572868
Sparse Core Ops, SparseCore 0:
  9.5 69.6 all-gather.2
  81.3 53.1 all-gather.4

commit v3 on v2

v3 whole, which is shorter than its diff:
```python
import functools
import math

import jax
import jax.numpy as jnp
from jax import lax
from jax.experimental import pallas as pl
from jax.experimental.pallas import tpu as pltpu
from jax.sharding import PartitionSpec as P

D = 2048
HD = 128
SLOT = 64
RANK = 64
GRP = 4
TOK = GRP * SLOT
K = 12
REQ_COL = 4

eps = 1e-12
lowrank_scale = 0.5

MESH = pl.DeviceIdType.MESH
HBM = pl.BlockSpec(memory_space=pl.ANY)
NT = (((1,), (1,)), ((), ()))
f32 = jnp.float32
bf16 = jnp.bfloat16


def dot(a, b):
    return jnp.dot(a, b, preferred_element_type=f32)


def dot_nt(a, b):
    return lax.dot_general(a, b, NT, preferred_element_type=f32)


def greet(peers):
    barrier = pltpu.get_barrier_semaphore()
    for peer in peers:
        pl.semaphore_signal(barrier, inc=1, device_id=peer, device_id_type=MESH)
    pl.semaphore_wait(barrier, len(peers))


class Sender:
    def __init__(self, send_sem, recv_sem):
        self.send_sem, self.recv_sem = send_sem, recv_sem
        self.copies = []

    def start(self, src, dst, peer):
        i = len(self.copies)
        copy = pltpu.make_async_remote_copy(
            src_ref=src,
            dst_ref=dst,
            send_sem=self.send_sem.at[i],
            recv_sem=self.recv_sem.at[i],
            device_id=peer,
            device_id_type=MESH,
        )
        copy.start()
        self.copies.append(copy)
        return copy


def row_place():
    row = lax.axis_index("row")
    col = lax.axis_index("col")
    z, core = row // 2, row % 2
    return row, col, z, core


def ring_gather(buf, row, col, z, core, sender):
    half = buf.shape[1] // 2
    up, down = (z + 1) % 4, (z + 3) % 4
    far = (z + 2) % 4

    def part(zz, h):
        return buf.at[zz * 2 + core, pl.ds(h * half, half)]

    def dev(zz):
        return (zz * 2 + core, col)

    partner = (z * 2 + 1 - core, col)
    a0 = sender.start(part(z, 0), part(z, 0), dev(up))
    b1 = sender.start(part(z, 1), part(z, 1), dev(down))
    a1 = sender.start(part(z, 1), part(z, 1), dev(up))
    b0 = sender.start(part(z, 0), part(z, 0), dev(down))
    own = sender.start(buf.at[row], buf.at[row], partner)
    rest = [own]

    def across(zz, h):
        rest.append(sender.start(part(zz, h), part(zz, h), partner))

    yield
    a0.wait_recv()
    r0 = sender.start(part(down, 0), part(down, 0), dev(up))
    across(down, 0)
    b1.wait_recv()
    r1 = sender.start(part(up, 1), part(up, 1), dev(down))
    across(up, 1)
    yield
    a1.wait_recv()
    across(down, 1)
    b0.wait_recv()
    across(up, 0)
    yield
    r0.wait_recv()
    across(far, 0)
    r1.wait_recv()
    across(far, 1)
    yield
    for copy in rest:
        copy.wait_recv()


def finish(run):
    for _ in run:
        pass


def row_neighbours(col, z, core):
    return [
        (((z + 1) % 4) * 2 + core, col),
        (((z + 3) % 4) * 2 + core, col),
        (z * 2 + 1 - core, col),
    ]


def torus_gather(src, dst, row, x, y, sender):
    rows = src.shape[0]
    half, quarter = rows // 2, rows // 4

    def step(p, d):
        return (p + d) % 4

    flows = []
    for first in (0, 1):
        base = first * half

        def at(a, b, first=first):
            return (a * 4 + b) if first == 0 else (b * 4 + a)

        p, q = (x, y) if first == 0 else (y, x)

        def dev(a, b, at=at):
            return (row, at(a, b))

        def blk(a, b, lo, n, at=at, base=base):
            return dst.at[at(a, b), pl.ds(base + lo, n)]

        own = src.at[pl.ds(base, half)]
        flows.append((p, q, dev, blk, own))

    state = []
    for p, q, dev, blk, own in flows:
        here = blk(p, q, 0, half)
        a = sender.start(own, here, dev(step(p, 1), q))
        b = sender.start(own, here, dev(step(p, 3), q))
        c = sender.start(own, here, dev(p, step(q, 1)))
        d = sender.start(own, here, dev(p, step(q, 3)))
        state.append([a, b, [(p, c, d)]])
    yield
    relays = []
    for (p, q, dev, blk, own), st in zip(flows, state):
        a, b, second = st
        lo, hi = step(p, 3), step(p, 1)
        a.wait_recv()
        v = blk(lo, q, 0, quarter)
        r0 = sender.start(v, v, dev(step(p, 1), q))
        v = blk(lo, q, 0, half)
        second.append(
            (lo, sender.start(v, v, dev(p, step(q, 1))), sender.start(v, v, dev(p, step(q, 3))))
        )
        b.wait_recv()
        v = blk(hi, q, quarter, quarter)
        r1 = sender.start(v, v, dev(step(p, 3), q))
        v = blk(hi, q, 0, half)
        second.append(
            (hi, sender.start(v, v, dev(p, step(q, 1))), sender.start(v, v, dev(p, step(q, 3))))
        )
        st.append((r0, r1))
    yield
    for (p, q, dev, blk, own), st in zip(flows, state):
        second, (r0, r1) = st[2], st[3]
        r0.wait_recv()
        r1.wait_recv()
        fa = step(p, 2)
        v = blk(fa, q, 0, half)
        second.append(
            (fa, sender.start(v, v, dev(p, step(q, 1))), sender.start(v, v, dev(p, step(q, 3))))
        )
    yield
    last = []
    for i in range(4):
        for (p, q, dev, blk, own), st in zip(flows, state):
            pa, c, d = st[2][i]
            c.wait_recv()
            v = blk(pa, step(q, 3), 0, quarter)
            last.append(sender.start(v, v, dev(p, step(q, 1))))
            d.wait_recv()
            v = blk(pa, step(q, 1), quarter, quarter)
            last.append(sender.start(v, v, dev(p, step(q, 3))))
    yield
    for copy in last:
        copy.wait_recv()


def torus_neighbours(row, x, y):
    return [
        (row, (x + 1) % 4 * 4 + y),
        (row, (x + 3) % 4 * 4 + y),
        (row, x * 4 + (y + 1) % 4),
        (row, x * 4 + (y + 3) % 4),
    ]


def entry_kernel(
    tok_ref, meta_ref, tok_out, meta_out, tok_send, tok_recv, meta_send, meta_recv, own_sem
):
    row = lax.axis_index("row")
    col = lax.axis_index("col")
    x, y = col // 4, col % 4
    peers = [(row, (col + i) % 16) for i in range(1, 16)]
    own = [
        pltpu.make_async_copy(tok_ref, tok_out.at[col], own_sem.at[0]),
        pltpu.make_async_copy(meta_ref, meta_out.at[col], own_sem.at[1]),
    ]
    for copy in own:
        copy.start()
    greet(peers)
    tok_sender = Sender(tok_send, tok_recv)
    meta_sender = Sender(meta_send, meta_recv)
    run = torus_gather(tok_ref, tok_out, row, x, y, tok_sender)
    next(run)
    for peer in peers:
        meta_sender.start(meta_ref, meta_out.at[col], peer)
    finish(run)
    for copy in meta_sender.copies:
        copy.wait_recv()
    for sender in (tok_sender, meta_sender):
        for copy in sender.copies:
            copy.wait_send()
    for copy in own:
        copy.wait()


def entry_gather(tok, meta):
    arrays = (tok, meta)
    return pl.pallas_call(
        entry_kernel,
        out_shape=[jax.ShapeDtypeStruct((16,) + a.shape, a.dtype) for a in arrays],
        in_specs=[HBM] * 2,
        out_specs=[HBM] * 2,
        scratch_shapes=[pltpu.SemaphoreType.DMA((40,))] * 2
        + [pltpu.SemaphoreType.DMA((15,))] * 2
        + [pltpu.SemaphoreType.DMA((2,))],
        compiler_params=pltpu.CompilerParams(collective_id=0, has_side_effects=True),
        name="entry_gather",
    )(tok, meta)


def exit_kernel(pick, in_ref, out_ref, send_sem, recv_sem, r_send, r_recv, own_sem, arrived):
    row, col, z, core = row_place()
    peers = [(col + i) % 16 for i in range(1, 16)]
    here = arrived.at[pl.ds(col * 2, 2)]
    own = pltpu.make_async_copy(in_ref.at[col], here, own_sem)
    own.start()
    greet([(row, c) for c in peers] + row_neighbours(col, z, core))
    sender = Sender(send_sem, recv_sem)
    for c in peers:
        sender.start(in_ref.at[c], here, (row, c))
    own.wait()
    for copy in sender.copies:
        copy.wait_recv()
    mine = jnp.concatenate([arrived[pick[i]] for i in range(REQ_COL)], axis=0)
    out_ref[row] = mine.T
    r_sender = Sender(r_send, r_recv)
    finish(ring_gather(out_ref, row, col, z, core, r_sender))
    for copy in sender.copies + r_sender.copies:
        copy.wait_send()


def send_home(packed, pick):
    return pl.pallas_call(
        exit_kernel,
        out_shape=jax.ShapeDtypeStruct((8, 256, TOK), packed.dtype),
        in_specs=[pl.BlockSpec(memory_space=pltpu.SMEM), HBM],
        out_specs=pl.BlockSpec(memory_space=pltpu.VMEM),
        scratch_shapes=[
            pltpu.SemaphoreType.DMA((15,)),
            pltpu.SemaphoreType.DMA((15,)),
            pltpu.SemaphoreType.DMA((13,)),
            pltpu.SemaphoreType.DMA((13,)),
            pltpu.SemaphoreType.DMA,
            pltpu.VMEM((32, SLOT, 256), packed.dtype),
        ],
        compiler_params=pltpu.CompilerParams(collective_id=1, has_side_effects=True),
        name="send_home",
    )(pick, packed)


def scatter_sum(part, theirs, sums, row, col, z, core, sender):
    half = TOK // 2
    top, bottom = pl.ds(0, half), pl.ds(half, half)
    partner = (z * 2 + 1 - core, col)
    up, down = (((z + 1) % 4) * 2 + core, col), (((z + 3) % 4) * 2 + core, col)
    order = [(z + 2) % 4, (z + 1) % 4, (z + 3) % 4, z]
    swaps = [
        sender.start(part.at[zz, 1 - core], theirs.at[i], partner) for i, zz in enumerate(order)
    ]
    yield
    sent = []
    for i, zz in enumerate(order):
        swaps[i].wait_recv()
        both = (theirs[i].astype(f32) + part[zz, core].astype(f32)).astype(bf16)
        if i == 3:
            sums[3] = both
            continue
        theirs[i] = both
        if i == 0:
            r0 = sender.start(theirs.at[0, top], sums.at[4, top], up)
            r1 = sender.start(theirs.at[0, bottom], sums.at[4, bottom], down)
        else:
            sent.append(sender.start(theirs.at[i], sums.at[i], up if i == 1 else down))
    yield
    r0.wait_recv()
    sent.append(sender.start(sums.at[4, top], sums.at[0, top], up))
    r1.wait_recv()
    sent.append(sender.start(sums.at[4, bottom], sums.at[0, bottom], down))
    yield
    for copy in sent:
        copy.wait_recv()


def stat_exchange(stats, row, col, sender):
    copies = [
        sender.start(stats.at[row], stats.at[row], ((row + i) % 8, col)) for i in range(1, 8)
    ]
    yield
    for copy in copies:
        copy.wait_recv()


def slot_rows(i):
    return slice(i * SLOT, (i + 1) * SLOT)


def rank_sum(buf, first):
    total = buf[0, first : first + RANK, :].astype(f32)
    for r in range(1, 8):
        total = total + buf[r, first : first + RANK, :].astype(f32)
    return total.astype(bf16)


def weight_rows(weight, r):
    return weight[2 * r : 2 * r + 2].reshape(256, weight.shape[2])


def project(buf, weight):
    base = dot(buf[0, :TOK, :], weight_rows(weight, 0))
    for r in range(1, 8):
        base = base + dot(buf[r, :TOK, :], weight_rows(weight, r))
    return base


def gelu(v):
    return 0.5 * v * (1.0 + jnp.tanh(math.sqrt(2.0 / math.pi) * (v + 0.044715 * (v * v * v))))


def stats_of(values):
    lane = lax.broadcasted_iota(jnp.int32, (TOK, 128), 1)
    one = jnp.sum(values, axis=1, keepdims=True)
    two = jnp.sum(values * values, axis=1, keepdims=True)
    flipped = jnp.where(lane < 64, one, two).T
    return jnp.concatenate([flipped[0:8], flipped[64:72]], axis=0)


def norm_of(values, stats, gain, shift):
    total = stats[0]
    for r in range(1, 8):
        total = total + stats[r]
    total = total * (1.0 / D)
    mean = total[0:1, :]
    square = total[8:9, :]
    factor = lax.rsqrt(square - mean * mean + eps)
    both = jnp.concatenate(
        [
            jnp.broadcast_to(mean, (8, TOK)),
            jnp.broadcast_to(factor, (8, TOK)),
            jnp.zeros((112, TOK), f32),
        ],
        axis=0,
    ).T
    return (values - both[:, 0:1]) * both[:, 8:9] * gain + shift


GROUPS = K // GRP
HIGH = TOK + 3 * RANK
LOW = TOK + RANK
STORES = 8


def wave_kernel(*refs):
    table, vectors = refs[0], refs[1]
    tok_hbm = refs[2]
    weight_hbm = refs[3:7]
    store_hbm = refs[7 : 7 + STORES]
    out = refs[15]
    toks = refs[16]
    weights = refs[17:21]
    stores = refs[21 : 21 + STORES]
    buf1, buf2, buf3, bufu, part, theirs, sums, pre, stats = refs[29:38]
    load_sem, ring_send, ring_recv, torus_send, torus_recv = refs[38:43]
    swap_send, swap_recv, stat_send, stat_recv = refs[43:47]
    a_shrink, a_expand, o_shrink, o_expand, u_shrink, u_expand, d_shrink, d_expand = stores

    row, col, z, core = row_place()
    x, y = col // 4, col % 4
    loads = [pltpu.make_async_copy(tok_hbm, toks, load_sem.at[0])]
    for i in range(STORES):
        loads.append(pltpu.make_async_copy(store_hbm[i], stores[i], load_sem.at[1 + i]))
    for i in range(4):
        loads.append(
            pltpu.make_async_copy(weight_hbm[i], weights[i].at[col], load_sem.at[9 + i])
        )
    for copy in loads:
        copy.start()
    greet([((row + i) % 8, col) for i in range(1, 8)] + torus_neighbours(row, x, y))

    senders = []

    def sender(send, recv, i):
        senders.append(Sender(send.at[i], recv.at[i]))
        return senders[-1]

    def ring(buf, i):
        return ring_gather(buf, row, col, z, core, sender(ring_send, ring_recv, i))

    each = range(GROUPS)
    r1 = [ring(buf1.at[g], g) for g in each]
    r2 = [ring(buf2.at[g], GROUPS + g) for g in each]
    r3 = [ring(buf3.at[g], 2 * GROUPS + g) for g in each]
    ru = [ring(bufu.at[g], 3 * GROUPS + g) for g in each]
    tq, to, tw, tc = [
        torus_gather(weight_hbm[i], weights[i], row, x, y, sender(torus_send, torus_recv, i))
        for i in range(4)
    ]
    xs = [
        scatter_sum(
            part.at[g], theirs.at[g], sums.at[g], row, col, z, core,
            sender(swap_send, swap_recv, g),
        )
        for g in each
    ]
    s1 = [stat_exchange(stats.at[g], row, col, sender(stat_send, stat_recv, g)) for g in each]
    s2 = [
        stat_exchange(
            stats.at[GROUPS + g], row, col, sender(stat_send, stat_recv, GROUPS + g)
        )
        for g in each
    ]
    waited = set()

    def loaded(*which):
        for i in which:
            if i not in waited:
                waited.add(i)
                loads[i].wait()

    def go(*runs):
        for run in runs:
            next(run, None)

    first_slot = table[3, 0]

    def entry(kind, g, i):
        return table[kind, first_slot + (g * GRP + i)]

    def pack(g):
        loaded(0, 1)
        for i in range(GRP):
            v = toks[entry(0, g, i)]
            buf1[g, row, slot_rows(i), :] = v
            u = dot_nt(v, a_shrink[entry(1, g, i)]).astype(bf16)
            for j in range(3):
                buf1[g, row, TOK + j * RANK : TOK + (j + 1) * RANK, slot_rows(i)] = u[
                    :, j * RANK : (j + 1) * RANK
                ]

    def attend(g):
        loaded(2, 3, 9)
        buf = buf1.at[g]
        base = project(buf, weights[0])
        reduced = [rank_sum(buf, TOK + j * RANK) for j in range(3)]
        lane = lax.broadcasted_iota(jnp.int32, (SLOT, SLOT), 1)
        for i in range(GRP):
            at = entry(1, g, i)
            deltas = [
                dot(reduced[j][:, slot_rows(i)], a_expand[at, j]).astype(bf16).astype(f32)
                for j in range(3)
            ]
            valid = lane < entry(2, g, i)
            contexts = []
            for h in range(2):
                q, k, v = [
                    (
                        base[slot_rows(i), h * 384 + j * HD : h * 384 + (j + 1) * HD]
                        + lowrank_scale * deltas[j][:, h * HD : (h + 1) * HD]
                    ).astype(bf16)
                    for j in range(3)
                ]
                scores = dot_nt(q, k) / math.sqrt(HD)
                weight = jnp.where(valid, jnp.exp(scores), 0.0)
                probs = (weight / jnp.sum(weight, axis=1, keepdims=True)).astype(bf16)
                contexts.append(dot(probs, v).astype(bf16))
            context = jnp.concatenate(contexts, axis=1)
            buf2[g, row, slot_rows(i), :] = context
            buf2[g, row, TOK:LOW, slot_rows(i)] = dot_nt(context, o_shrink[at]).astype(bf16)

    def add_delta(g, reduced, expand, residual, base):
        for i in range(GRP):
            delta = dot(reduced[:, slot_rows(i)], expand[entry(1, g, i)])
            pre[g, slot_rows(i), :] = (
                residual[row, slot_rows(i), :].astype(f32)
                + base[slot_rows(i), :]
                + lowrank_scale * delta.astype(bf16).astype(f32)
            )

    def mix(g):
        loaded(4, 10)
        add_delta(g, rank_sum(buf2.at[g], TOK), o_expand, buf1.at[g], project(buf2.at[g], weights[1]))
        stats[g, row] = stats_of(pre[g])

    def first(g):
        loaded(5)
        v = norm_of(pre[g], stats.at[g], vectors[0:1], vectors[1:2]).astype(bf16)
        buf3[g, row, :TOK, :] = v
        for i in range(GRP):
            buf3[g, row, TOK:LOW, slot_rows(i)] = dot_nt(
                v[slot_rows(i), :], u_shrink[entry(1, g, i)]
            ).astype(bf16)

    def hidden(g):
        loaded(6, 7, 11, 12)
        base = project(buf3.at[g], weights[2])
        reduced = rank_sum(buf3.at[g], TOK)
        rows = []
        for i in range(GRP):
            at = entry(1, g, i)
            delta = dot(reduced[:, slot_rows(i)], u_expand[at]).astype(bf16).astype(f32)
            unit = gelu(base[slot_rows(i), :] + lowrank_scale * delta).astype(bf16)
            rows.append(unit)
            bufu[g, row, :, slot_rows(i)] = dot_nt(unit, d_shrink[at]).astype(bf16)
        units = jnp.concatenate(rows, axis=0)
        for r in range(8):
            part[g, r // 2, r % 2] = dot_nt(units, weight_rows(weights[3], r)).astype(bf16)

    def second(g):
        loaded(8)
        base = sums[g, 0].astype(f32)
        for r in range(1, 4):
            base = base + sums[g, r].astype(f32)
        add_delta(g, rank_sum(bufu.at[g], 0), d_expand, buf3.at[g], base)
        stats[GROUPS + g, row] = stats_of(pre[g])

    def last(g):
        v = norm_of(pre[g], stats.at[GROUPS + g], vectors[2:3], vectors[3:4])
        out[g * TOK : (g + 1) * TOK, :] = v.astype(bf16)

    go(tq)
    pack(0)
    go(r1[0])
    pack(1)
    go(tq, r1[0], r1[1])
    pack(2)
    go(tq, r1[0], r1[1], r1[0], r1[2], tq, to, r1[1], r1[0], tq)
    attend(0)
    go(r2[0], to, to, tw, r1[1], r1[2], r1[2], r2[0], r1[1])
    attend(1)
    go(r2[1], to, tw, r1[2], r2[0], r1[2])
    attend(2)
    go(r2[2], r2[0], r2[1], tw, tc, to, r2[1], r2[0])
    mix(0)
    go(s1[0], r2[1], r2[2], r2[2], tw, tc, r2[1])
    mix(1)
    go(s1[1], s1[0])
    first(0)
    go(r3[0], r2[2], tc, r2[2])
    mix(2)
    go(s1[2], s1[1])
    first(1)
    go(r3[0], r3[1], s1[2])
    first(2)
    go(tc, r3[0], r3[1], r3[0], r3[2], r3[1], r3[0], tw, tc)
    hidden(0)
    go(xs[0], ru[0], r3[1], r3[2], r3[2], r3[1])
    hidden(1)
    go(xs[1], ru[1], xs[0], ru[0], r3[2], r3[2], xs[0])
    hidden(2)
    go(xs[2], ru[2], xs[1], ru[1], xs[0], ru[0], ru[0], ru[0], xs[1], xs[2], ru[2])
    second(0)
    go(s2[0], ru[1], ru[1], xs[2], xs[1], ru[1])
    second(1)
    go(s2[1], s2[0])
    last(0)
    go(ru[2], ru[2], xs[2], ru[2])
    second(2)
    go(s2[2], s2[1])
    last(1)
    go(s2[2])
    last(2)
    for run in r1 + r2 + r3 + ru + [tq, to, tw, tc] + xs + s1 + s2:
        assert next(run, row) is row
    for one in senders:
        for copy in one.copies:
            copy.wait_send()


def run_wave(table, vectors, toks, base_weights, stores):
    vmem = pl.BlockSpec(memory_space=pltpu.VMEM)
    dma = pltpu.SemaphoreType.DMA
    rings = 4 * GROUPS
    return pl.pallas_call(
        wave_kernel,
        out_shape=jax.ShapeDtypeStruct((K * SLOT, 256), bf16),
        in_specs=[pl.BlockSpec(memory_space=pltpu.SMEM), vmem] + [HBM] * 13,
        out_specs=vmem,
        scratch_shapes=[pltpu.VMEM(toks.shape, bf16)]
        + [pltpu.VMEM((16,) + w.shape, bf16) for w in base_weights]
        + [pltpu.VMEM(s.shape, bf16) for s in stores]
        + [
            pltpu.VMEM((GROUPS, 8, HIGH, 256), bf16),
            pltpu.VMEM((GROUPS, 8, LOW, 256), bf16),
            pltpu.VMEM((GROUPS, 8, LOW, 256), bf16),
            pltpu.VMEM((GROUPS, 8, RANK, 256), bf16),
            pltpu.VMEM((GROUPS, 4, 2, TOK, 256), bf16),
            pltpu.VMEM((GROUPS, 4, TOK, 256), bf16),
            pltpu.VMEM((GROUPS, 5, TOK, 256), bf16),
            pltpu.VMEM((GROUPS, TOK, 256), f32),
            pltpu.VMEM((2 * GROUPS, 8, 16, 256), f32),
        ]
        + [dma((13,)), dma((rings, 13)), dma((rings, 13)), dma((4, 40)), dma((4, 40))]
        + [dma((GROUPS, 10)), dma((GROUPS, 10)), dma((2 * GROUPS, 7)), dma((2 * GROUPS, 7))],
        compiler_params=pltpu.CompilerParams(
            collective_id=2, has_side_effects=True, vmem_limit_bytes=67043328
        ),
        name="wave",
    )(table, vectors, toks, *base_weights, *stores)


def shards(
    tokens,
    lengths,
    adapter_ids,
    adapter_place,
    attention_qkv_weight,
    attention_out_weight,
    widen_weight,
    contract_weight,
    first_gain,
    first_shift,
    second_gain,
    second_shift,
    *stores,
):
    i32 = jnp.int32
    col = lax.axis_index("col")
    row = lax.axis_index("row")
    stored = stores[0].shape[0]
    match = adapter_ids[:, None] == jnp.arange(adapter_place.shape[0], dtype=i32)[None, :]
    position = jnp.sum(jnp.where(match, adapter_place[None, :], 0), axis=1)
    meta = jnp.zeros((8, 128), i32)
    meta = meta.at[0, :REQ_COL].set(position).at[1, :REQ_COL].set(lengths)
    tok_all, meta_all = entry_gather(tokens.T, meta)
    tok_all = tok_all.reshape(64, SLOT, 256)

    requests = 64
    position = meta_all[:, 0, :REQ_COL].reshape(requests)
    length = meta_all[:, 1, :REQ_COL].reshape(requests)
    owner, local = position // stored, position % stored
    n = jnp.arange(requests, dtype=i32)
    same = (owner[None, :] == owner[:, None]) & (n[None, :] < n[:, None])
    rank = jnp.sum(same.astype(i32), axis=1)
    near = jnp.sum((same & (n[None, :] // REQ_COL == n[:, None] // REQ_COL)).astype(i32), axis=1)
    waves = (jnp.max(rank) + K) // K
    most = -(-32 // K)
    slots = jnp.arange(most * K, dtype=i32)
    mine = owner == col
    hit = mine[None, :] & (rank[None, :] == slots[:, None])
    facts = jnp.stack([n, local, length - 1])
    table = jnp.sum(jnp.where(hit[None], facts[:, None, :], 0), axis=2)
    table = table + jnp.array([[0], [0], [1]], i32)
    pair = jnp.arange(32, dtype=i32)
    out_hit = mine[None, :] & ((n // REQ_COL * 2 + near)[None, :] == pair[:, None])
    out_slot = jnp.sum(jnp.where(out_hit, rank[None, :], 0), axis=1)
    home_n = col * REQ_COL + jnp.arange(REQ_COL, dtype=i32)
    home_hit = home_n[:, None] == n[None, :]
    home_from = jnp.sum(jnp.where(home_hit, (owner * 2 + near)[None, :], 0), axis=1)
    tail = [lax.dynamic_slice_in_dim(v, row * 256, 256, 0) for v in (first_shift, second_gain, second_shift)]
    vectors = jnp.stack([first_gain] + tail)
    base_weights = (attention_qkv_weight, attention_out_weight, widen_weight, contract_weight)

    def wave(w, held):
        with_start = jnp.concatenate([table, jnp.full((1, most * K), w * K, i32)])
        result = run_wave(with_start, vectors, tok_all, base_weights, stores)
        return lax.dynamic_update_index_in_dim(held, result, w, 0)

    held = lax.fori_loop(0, waves, wave, jnp.zeros((most, K * SLOT, 256), bf16))
    packed = jnp.take(held.reshape(most * K, SLOT, 256), out_slot, axis=0)
    return send_home(packed.reshape(16, 2, SLOT, 256), home_from).reshape(D, TOK)


def solution(mesh):
    return jax.shard_map(
        shards,
        mesh=mesh,
        in_specs=(
            P("row", "col"),
            P("col"),
            P("col"),
            P(),
            P("col", "row"),
            P("col", "row"),
            P("col", "row"),
            P("col", "row"),
            P("row"),
            P(),
            P(),
            P(),
            P("col", None, "row"),
            P("col", None, None, "row"),
            P("col", None, "row"),
            P("col", None, "row"),
            P("col", None, "row"),
            P("col", None, "row"),
            P("col", None, "row"),
            P("col", None, "row"),
        ),
        out_specs=P(None, "col"),
        check_vma=False,
    )
```

time: 286 us -> 216 us (0.76); the launches traced: 281 us -> 215 us
  Pallas kernels: 253 us -> 191 us
  between operations: 14.4 us -> 0.8 us
  other arithmetic: 2.91 us -> 8.69 us
  local copies, waits for them, and re-layouts: 9.58 us -> 14 us
    pallas_call x13 -> x1, Pallas kernels: 201 us -> 142 us  [run_wave(): pl.pallas_call(wave_kernel, out_shape=jax.ShapeDtypeStruct((K * SLOT, 256...]
    pallas_call x1, Pallas kernels: 23.8 us -> 20.8 us  [entry_gather(): pl.pallas_call(entry_kernel, out_shape=[jax.ShapeDtypeStruct((16,) + a.sh...]
  transfers between devices with their start and end apart: 2 -> 0, of which waited for: 0 -> 0; matrix products, arithmetic and copies ran while one was open for 3% -> 0% of each run, Pallas kernels for 58% -> 0%
where the time goes in v3:
time: 216 us; the launch traced here: 215 us
  Pallas kernels  191 us (88%)
  local copies, waits for them, and re-layouts  14 us (6%)
  other arithmetic  8.69 us (4%)
    pallas_call x1, Pallas kernels, run_wave(): pl.pallas_call(wave_kernel, out_shape=jax.ShapeDtypeStruct((K * SLOT, 256...  142 us
    pallas_call x1, Pallas kernels, send_home(): pl.pallas_call(exit_kernel, out_shape=jax.ShapeDtypeStruct((8, 256, TOK),...  28.4 us
    pallas_call x1, Pallas kernels, entry_gather(): pl.pallas_call(entry_kernel, out_shape=[jax.ShapeDtypeStruct((16,) + a.sh...  20.8 us
    unnamed x8, local copies, waits for them, and re-layouts  4.52 us

profile of v3, /device:TPU:1, one launch (start us, length us, event | category | flops | bytes accessed | tf_op | source)
XLA Modules:
  0.0 214.6 jit_solution(746203643584020344)
XLA Ops:
  0.0 1.7 copy.24
  1.7 0.9 select_reduce_fusion.2
  2.5 0.8 scatter.9.meta_ref
  3.3 0.0 copy-start
  3.3 0.6 copy-done
  3.9 20.8 %entry_gather.1 = (bf16[16,256,256]{2,1,0:T(8,128)(2,1)}, s32[16,8,128]{2,1,0:T(8,128)}) custom-call(bf16[256,256]{1,0:T(8,128)(2,1)} %bitcast.24, s32[8,128]{1,0:T(8,128)} %copy-done), custom_call_target="tpu_custom_call" | custom-call | tf_op jit(solution)/shard_map/entry_gather/pallas_call | solution.py:249
  24.8 1.0 add_reduce_fusion
  25.7 0.1 reshape_squeeze.6
  25.9 0.2 convert_reduce_fusion
  26.0 0.5 multiply_add_fusion
  26.6 0.8 select_reduce_fusion.3.pick
  27.3 0.6 reduce_max.9
  28.6 0.1 sub.34
  28.7 0.1 reshape_squeeze.7
  28.9 0.1 select_reduce_fusion
  29.0 1.3 broadcast_add_fusion
  30.3 0.0 copy-done.1
  30.3 0.8 dynamic_slice.11
  31.1 0.8 dynamic_slice.10
  31.9 0.8 dynamic_slice.9
  32.6 1.3 pad_maximum_fusion
  33.9 1.1 broadcast_in_dim.103
  35.0 145.0 %while.12 = (s32[]{:T(128)}, bf16[3,768,256]{2,1,0:T(8,128)(2,1)}, s32[]{:T(128)}, s32[3,36]{1,0:T(4,128)}, f32[4,256]{1,0:T(4,128)}, /*index=5*/bf16[64,64,256]...) while((s32[]{:T(128)}, bf16[3,768,256]{2,1,0:T(8,128)(2,1)}, ...), condition=%wide.region_8.9_spmd, body=%wide.region_7.8_spmd.sunk | while | flops 6 | bytes 787699 | solution.py:708
  35.0 1.3 concatenate.8.refs_0_
  36.3 141.9 %wave.1 = bf16[768,256]{1,0:T(8,128)(2,1)} custom-call(s32[4,36]{1,0:T(4,128)} %concatenate.8.refs_0_, f32[4,256]{1,0:T(4,128)} %get-tuple-element.330.refs_1_, bf16[64,64,256]{2,1,0:T(8,128)(2,1)} %get-tuple-element.331.refs_2_, bf16[128,768]{1,0:T(8,128)(2,1)} %get-tuple-element.332.refs_3_, bf16[128,256]{1,0:T(8,128)(2,1)} %get-tuple-element.333.refs_4_, ...), custom_call_target="tpu_custom_call" | custom-call | tf_op jit(solution)/shard_map/while/body/wave/pallas_call | solution.py:623
  178.2 1.8 bitcast_dynamic-update-slice_fusion.2
  180.0 0.8 select_reduce_fusion.1
  180.9 1.9 gather_fusion
  182.7 0.1 reduce_sum.63
  182.8 1.1 broadcast_select_fusion.in_ref
  184.0 28.4 %send_home.1 = bf16[8,256,256]{2,1,0:T(8,128)(2,1)} custom-call(s32[4]{0:T(128)} %select_reduce_fusion.3.pick, bf16[16,2,64,256]{3,2,1,0:T(8,128)(2,1)} %broadcast_select_fusion.in_ref), custom_call_target="tpu_custom_call" | custom-call | tf_op jit(solution)/shard_map/send_home/pallas_call | solution.py:284
  212.4 2.3 %copy.34 = bf16[2048,256]{1,0:T(8,128)(2,1)} copy(bf16[2048,256]{1,0:T(8,128)(2,1)} %bitcast.23) | data formatting | bytes 2097152
  (14 shorter events, 0.1 us)
Async XLA Ops:
  3.3 0.6 copy-start
  25.8 4.5 %copy-start.1 = (pred[64]{0:T(512)(128)(4,1)}, pred[64]{0:T(512)(128)(4,1)S(1)}, u32[]{:S(2)}) copy-start(pred[64]{0:T(512)(128)(4,1)S(1)} %get-tuple-element.167) | copy-start | bytes 196
  26.0 4.3 %copy-start.2 = (s32[64]{0:T(128)}, s32[64]{0:T(128)S(1)}, u32[]{:S(2)}) copy-start(s32[64]{0:T(128)S(1)} %get-tuple-element.129) | copy-start | bytes 772

commit v4 on v3

--- a/solution.py
+++ b/solution.py
@@ -259,46 +259,6 @@
     )(tok, meta)
 
 
-def exit_kernel(pick, in_ref, out_ref, send_sem, recv_sem, r_send, r_recv, own_sem, arrived):
-    row, col, z, core = row_place()
-    peers = [(col + i) % 16 for i in range(1, 16)]
-    here = arrived.at[pl.ds(col * 2, 2)]
-    own = pltpu.make_async_copy(in_ref.at[col], here, own_sem)
-    own.start()
-    greet([(row, c) for c in peers] + row_neighbours(col, z, core))
-    sender = Sender(send_sem, recv_sem)
-    for c in peers:
-        sender.start(in_ref.at[c], here, (row, c))
-    own.wait()
-    for copy in sender.copies:
-        copy.wait_recv()
-    mine = jnp.concatenate([arrived[pick[i]] for i in range(REQ_COL)], axis=0)
-    out_ref[row] = mine.T
-    r_sender = Sender(r_send, r_recv)
-    finish(ring_gather(out_ref, row, col, z, core, r_sender))
-    for copy in sender.copies + r_sender.copies:
-        copy.wait_send()
-
-
-def send_home(packed, pick):
-    return pl.pallas_call(
-        exit_kernel,
-        out_shape=jax.ShapeDtypeStruct((8, 256, TOK), packed.dtype),
-        in_specs=[pl.BlockSpec(memory_space=pltpu.SMEM), HBM],
-        out_specs=pl.BlockSpec(memory_space=pltpu.VMEM),
-        scratch_shapes=[
-            pltpu.SemaphoreType.DMA((15,)),
-            pltpu.SemaphoreType.DMA((15,)),
-            pltpu.SemaphoreType.DMA((13,)),
-            pltpu.SemaphoreType.DMA((13,)),
-            pltpu.SemaphoreType.DMA,
-            pltpu.VMEM((32, SLOT, 256), packed.dtype),
-        ],
-        compiler_params=pltpu.CompilerParams(collective_id=1, has_side_effects=True),
-        name="send_home",
-    )(pick, packed)
-
-
 def scatter_sum(part, theirs, sums, row, col, z, core, sender):
     half = TOK // 2
     top, bottom = pl.ds(0, half), pl.ds(half, half)
@@ -309,7 +269,7 @@
         sender.start(part.at[zz, 1 - core], theirs.at[i], partner) for i, zz in enumerate(order)
     ]
     yield
-    sent = []
+    far, sent = [], []
     for i, zz in enumerate(order):
         swaps[i].wait_recv()
         both = (theirs[i].astype(f32) + part[zz, core].astype(f32)).astype(bf16)
@@ -318,15 +278,18 @@
             continue
         theirs[i] = both
         if i == 0:
-            r0 = sender.start(theirs.at[0, top], sums.at[4, top], up)
-            r1 = sender.start(theirs.at[0, bottom], sums.at[4, bottom], down)
+            far.append(sender.start(theirs.at[0, top], sums.at[0, top], up))
+            far.append(sender.start(theirs.at[0, bottom], sums.at[0, bottom], down))
+        elif i == 1:
+            sent.append(sender.start(theirs.at[1, bottom], sums.at[1, bottom], up))
         else:
-            sent.append(sender.start(theirs.at[i], sums.at[i], up if i == 1 else down))
-    yield
-    r0.wait_recv()
-    sent.append(sender.start(sums.at[4, top], sums.at[0, top], up))
-    r1.wait_recv()
-    sent.append(sender.start(sums.at[4, bottom], sums.at[0, bottom], down))
+            sent.append(sender.start(theirs.at[2, top], sums.at[2, top], down))
+    yield
+    for i, rows, peer in ((1, top, up), (2, bottom, down)):
+        far[i - 1].wait_recv()
+        merged = theirs[i, rows].astype(f32) + sums[0, rows].astype(f32)
+        theirs[i, rows] = merged.astype(bf16)
+        sent.append(sender.start(theirs.at[i, rows], sums.at[i, rows], peer))
     yield
     for copy in sent:
         copy.wait_recv()
@@ -394,25 +357,27 @@
     return (values - both[:, 0:1]) * both[:, 8:9] * gain + shift
 
 
-GROUPS = K // GRP
 HIGH = TOK + 3 * RANK
 LOW = TOK + RANK
 STORES = 8
 
 
-def wave_kernel(*refs):
-    table, vectors = refs[0], refs[1]
-    tok_hbm = refs[2]
-    weight_hbm = refs[3:7]
-    store_hbm = refs[7 : 7 + STORES]
-    out = refs[15]
-    toks = refs[16]
-    weights = refs[17:21]
-    stores = refs[21 : 21 + STORES]
-    buf1, buf2, buf3, bufu, part, theirs, sums, pre, stats = refs[29:38]
-    load_sem, ring_send, ring_recv, torus_send, torus_recv = refs[38:43]
-    swap_send, swap_recv, stat_send, stat_recv = refs[43:47]
+def wave_kernel(groups, *refs):
+    start, table = refs[0], refs[1]
+    gain1, shift1, gain2, shift2 = refs[2:6]
+    out_hbm, tok_hbm = refs[6], refs[7]
+    weight_hbm = refs[8:12]
+    store_hbm = refs[12 : 12 + STORES]
+    out = refs[20]
+    toks = refs[21]
+    weights = refs[22:26]
+    stores = refs[26 : 26 + STORES]
+    buf1, buf2, buf3, bufu, part, theirs, sums, pre, stats = refs[34:43]
+    result, packed, arrived, held = refs[43:47]
+    load_sem, ring_send, ring_recv, torus_send, torus_recv = refs[47:52]
+    swap_send, swap_recv, stat_send, stat_recv, exit_send, exit_recv = refs[52:58]
     a_shrink, a_expand, o_shrink, o_expand, u_shrink, u_expand, d_shrink, d_expand = stores
+    slots = groups * GRP
 
     row, col, z, core = row_place()
     x, y = col // 4, col % 4
@@ -423,9 +388,15 @@
         loads.append(
             pltpu.make_async_copy(weight_hbm[i], weights[i].at[col], load_sem.at[9 + i])
         )
-    for copy in loads:
-        copy.start()
-    greet([((row + i) % 8, col) for i in range(1, 8)] + torus_neighbours(row, x, y))
+    loads.append(pltpu.make_async_copy(out.at[row], held, load_sem.at[13]))
+    columns = [(col + i) % 16 for i in range(1, 16)]
+
+    def begin(*which):
+        for i in which:
+            loads[i].start()
+
+    begin(0, 1, 9)
+    greet([((row + i) % 8, col) for i in range(1, 8)] + [(row, c) for c in columns])
 
     senders = []
 
@@ -436,11 +407,12 @@
     def ring(buf, i):
         return ring_gather(buf, row, col, z, core, sender(ring_send, ring_recv, i))
 
-    each = range(GROUPS)
+    each = range(groups)
     r1 = [ring(buf1.at[g], g) for g in each]
-    r2 = [ring(buf2.at[g], GROUPS + g) for g in each]
-    r3 = [ring(buf3.at[g], 2 * GROUPS + g) for g in each]
-    ru = [ring(bufu.at[g], 3 * GROUPS + g) for g in each]
+    r2 = [ring(buf2.at[g], groups + g) for g in each]
+    r3 = [ring(buf3.at[g], 2 * groups + g) for g in each]
+    ru = [ring(bufu.at[g], 3 * groups + g) for g in each]
+    rx = ring(out, 4 * groups)
     tq, to, tw, tc = [
         torus_gather(weight_hbm[i], weights[i], row, x, y, sender(torus_send, torus_recv, i))
         for i in range(4)
@@ -455,7 +427,7 @@
     s1 = [stat_exchange(stats.at[g], row, col, sender(stat_send, stat_recv, g)) for g in each]
     s2 = [
         stat_exchange(
-            stats.at[GROUPS + g], row, col, sender(stat_send, stat_recv, GROUPS + g)
+            stats.at[groups + g], row, col, sender(stat_send, stat_recv, groups + g)
         )
         for g in each
     ]
@@ -467,14 +439,13 @@
                 waited.add(i)
                 loads[i].wait()
 
-    def go(*runs):
-        for run in runs:
-            next(run, None)
-
-    first_slot = table[3, 0]
+    first_slot = start[0]
 
     def entry(kind, g, i):
         return table[kind, first_slot + (g * GRP + i)]
+
+    def own_features(ref):
+        return ref[:, pl.ds(pl.multiple_of(row * 256, 256), 256)]
 
     def pack(g):
         loaded(0, 1)
@@ -533,15 +504,17 @@
 
     def first(g):
         loaded(5)
-        v = norm_of(pre[g], stats.at[g], vectors[0:1], vectors[1:2]).astype(bf16)
+        v = norm_of(pre[g], stats.at[g], gain1[...], own_features(shift1)).astype(bf16)
         buf3[g, row, :TOK, :] = v
         for i in range(GRP):
             buf3[g, row, TOK:LOW, slot_rows(i)] = dot_nt(
                 v[slot_rows(i), :], u_shrink[entry(1, g, i)]
             ).astype(bf16)
 
-    def hidden(g):
-        loaded(6, 7, 11, 12)
+    units = {}
+
+    def rise(g):
+        loaded(6, 7, 11)
         base = project(buf3.at[g], weights[2])
         reduced = rank_sum(buf3.at[g], TOK)
         rows = []
@@ -551,101 +524,129 @@
             unit = gelu(base[slot_rows(i), :] + lowrank_scale * delta).astype(bf16)
             rows.append(unit)
             bufu[g, row, :, slot_rows(i)] = dot_nt(unit, d_shrink[at]).astype(bf16)
-        units = jnp.concatenate(rows, axis=0)
+        units[g] = jnp.concatenate(rows, axis=0)
+
+    def fall(g):
+        loaded(12)
         for r in range(8):
-            part[g, r // 2, r % 2] = dot_nt(units, weight_rows(weights[3], r)).astype(bf16)
+            part[g, r // 2, r % 2] = dot_nt(units[g], weight_rows(weights[3], r)).astype(bf16)
 
     def second(g):
         loaded(8)
-        base = sums[g, 0].astype(f32)
-        for r in range(1, 4):
-            base = base + sums[g, r].astype(f32)
+        base = sums[g, 1].astype(f32) + sums[g, 2].astype(f32) + sums[g, 3].astype(f32)
         add_delta(g, rank_sum(bufu.at[g], 0), d_expand, buf3.at[g], base)
-        stats[GROUPS + g, row] = stats_of(pre[g])
+        stats[groups + g, row] = stats_of(pre[g])
 
     def last(g):
-        v = norm_of(pre[g], stats.at[GROUPS + g], vectors[2:3], vectors[3:4])
-        out[g * TOK : (g + 1) * TOK, :] = v.astype(bf16)
-
-    go(tq)
-    pack(0)
-    go(r1[0])
-    pack(1)
-    go(tq, r1[0], r1[1])
-    pack(2)
-    go(tq, r1[0], r1[1], r1[0], r1[2], tq, to, r1[1], r1[0], tq)
-    attend(0)
-    go(r2[0], to, to, tw, r1[1], r1[2], r1[2], r2[0], r1[1])
-    attend(1)
-    go(r2[1], to, tw, r1[2], r2[0], r1[2])
-    attend(2)
-    go(r2[2], r2[0], r2[1], tw, tc, to, r2[1], r2[0])
-    mix(0)
-    go(s1[0], r2[1], r2[2], r2[2], tw, tc, r2[1])
-    mix(1)
-    go(s1[1], s1[0])
-    first(0)
-    go(r3[0], r2[2], tc, r2[2])
-    mix(2)
-    go(s1[2], s1[1])
-    first(1)
-    go(r3[0], r3[1], s1[2])
-    first(2)
-    go(tc, r3[0], r3[1], r3[0], r3[2], r3[1], r3[0], tw, tc)
-    hidden(0)
-    go(xs[0], ru[0], r3[1], r3[2], r3[2], r3[1])
-    hidden(1)
-    go(xs[1], ru[1], xs[0], ru[0], r3[2], r3[2], xs[0])
-    hidden(2)
-    go(xs[2], ru[2], xs[1], ru[1], xs[0], ru[0], ru[0], ru[0], xs[1], xs[2], ru[2])
-    second(0)
-    go(s2[0], ru[1], ru[1], xs[2], xs[1], ru[1])
-    second(1)
-    go(s2[1], s2[0])
-    last(0)
-    go(ru[2], ru[2], xs[2], ru[2])
-    second(2)
-    go(s2[2], s2[1])
-    last(1)
-    go(s2[2])
-    last(2)
-    for run in r1 + r2 + r3 + ru + [tq, to, tw, tc] + xs + s1 + s2:
+        v = norm_of(
+            pre[g], stats.at[groups + g], own_features(gain2), own_features(shift2)
+        ).astype(bf16)
+        for i in range(GRP):
+            result[g * GRP + i] = v[slot_rows(i), :]
+
+    def leave():
+        @pl.loop(0, 32)
+        def _(p):
+            slot = table[3, p] - first_slot
+            packed[p] = result[jnp.minimum(jnp.maximum(slot, 0), slots - 1)]
+
+        one = Sender(exit_send, exit_recv)
+        senders.append(one)
+        here = pl.ds(col * 2, 2)
+        for c in columns:
+            one.start(packed.at[pl.ds(c * 2, 2)], arrived.at[here], (row, c))
+        arrived[here] = packed[here]
+        loaded(13)
+        lane = lax.broadcasted_iota(jnp.int32, (256, TOK), 1)
+        fresh = jnp.zeros((256, TOK), jnp.int32)
+        for i in range(REQ_COL):
+            slot = table[5, i] - first_slot
+            now = jnp.where((slot >= 0) & (slot < slots), 1, 0)
+            fresh = jnp.where(lane // SLOT == i, now, fresh)
+        for copy in one.copies:
+            copy.wait_recv()
+        mine = jnp.concatenate([arrived[table[4, i]] for i in range(REQ_COL)], axis=0)
+        flipped = mine.astype(f32).T
+        held[...] = jnp.where(fresh == 1, flipped, held[...].astype(f32)).astype(bf16)
+        store = pltpu.make_async_copy(held, out.at[row], load_sem.at[14])
+        store.start()
+        store.wait()
+
+    def go(*items):
+        for item in items:
+            if isinstance(item, tuple):
+                what, g = item
+                if g >= groups:
+                    continue
+                if callable(what):
+                    what(g)
+                    continue
+                item = what[g]
+            next(item, None)
+
+    go(tq, (pack, 0))
+    begin(*range(2, 9), 10, 11, 12, 13)
+    go((r1, 0), (pack, 1), tq, (r1, 0), (r1, 1), (pack, 2), tq, (r1, 0), (r1, 1), (r1, 0), (r1, 2))
+    go(tq, to, tw, (r1, 1), (r1, 0), tq, (attend, 0))
+    go((r2, 0), to, to, tw, (r1, 1), (r1, 2), (r1, 2), (r2, 0), (r1, 1), tc, (attend, 1))
+    go((r2, 1), to, tw, (r1, 2), (r2, 0), (r1, 2), (attend, 2))
+    go((r2, 2), (r2, 0), (r2, 1), tw, tc, to, (r2, 1), (r2, 0), (mix, 0))
+    go((s1, 0), (r2, 1), (r2, 2), (r2, 2), tc, (r2, 1), (mix, 1), (s1, 1), (s1, 0), (first, 0))
+    go((r3, 0), (r2, 2), tc, (r2, 2), (mix, 2), (s1, 2), (s1, 1), (first, 1))
+    go((r3, 0), (r3, 1), (s1, 2), (first, 2))
+    go((r3, 0), (r3, 1), (r3, 0), (r3, 2), (r3, 1), (r3, 0), tw, (rise, 0), tc, (fall, 0))
+    go((xs, 0), (ru, 0), (r3, 1), (r3, 2), (r3, 2), (r3, 1), (rise, 1), (fall, 1))
+    go((xs, 1), (ru, 1), (xs, 0), (ru, 0), (r3, 2), (r3, 2), (xs, 0), (rise, 2), (fall, 2))
+    go((xs, 2), (ru, 2), (xs, 1), (ru, 1), (xs, 0), (ru, 0), (ru, 0), (ru, 0), (xs, 1))
+    go((xs, 2), (ru, 2), (second, 0), (s2, 0), (ru, 1), (ru, 1), (xs, 2), (xs, 1), (ru, 1))
+    go((second, 1), (s2, 1), (s2, 0), (last, 0), (ru, 2), (ru, 2), (xs, 2), (ru, 2))
+    go((second, 2), (s2, 2), (s2, 1), (last, 1), (s2, 2), (last, 2))
+    leave()
+    finish(rx)
+    for run in r1 + r2 + r3 + ru + [rx, tq, to, tw, tc] + xs + s1 + s2:
         assert next(run, row) is row
     for one in senders:
         for copy in one.copies:
             copy.wait_send()
 
 
-def run_wave(table, vectors, toks, base_weights, stores):
+def run_wave(groups, start, table, vectors, out, toks, base_weights, stores):
+    smem = pl.BlockSpec(memory_space=pltpu.SMEM)
     vmem = pl.BlockSpec(memory_space=pltpu.VMEM)
     dma = pltpu.SemaphoreType.DMA
-    rings = 4 * GROUPS
+    rings = 4 * groups + 1
     return pl.pallas_call(
-        wave_kernel,
-        out_shape=jax.ShapeDtypeStruct((K * SLOT, 256), bf16),
-        in_specs=[pl.BlockSpec(memory_space=pltpu.SMEM), vmem] + [HBM] * 13,
-        out_specs=vmem,
+        functools.partial(wave_kernel, groups),
+        out_shape=jax.ShapeDtypeStruct(out.shape, out.dtype),
+        in_specs=[smem] * 2 + [vmem] * 4 + [HBM] * 14,
+        out_specs=HBM,
         scratch_shapes=[pltpu.VMEM(toks.shape, bf16)]
         + [pltpu.VMEM((16,) + w.shape, bf16) for w in base_weights]
         + [pltpu.VMEM(s.shape, bf16) for s in stores]
         + [
-            pltpu.VMEM((GROUPS, 8, HIGH, 256), bf16),
-            pltpu.VMEM((GROUPS, 8, LOW, 256), bf16),
-            pltpu.VMEM((GROUPS, 8, LOW, 256), bf16),
-            pltpu.VMEM((GROUPS, 8, RANK, 256), bf16),
-            pltpu.VMEM((GROUPS, 4, 2, TOK, 256), bf16),
-            pltpu.VMEM((GROUPS, 4, TOK, 256), bf16),
-            pltpu.VMEM((GROUPS, 5, TOK, 256), bf16),
-            pltpu.VMEM((GROUPS, TOK, 256), f32),
-            pltpu.VMEM((2 * GROUPS, 8, 16, 256), f32),
+            pltpu.VMEM((groups, 8, HIGH, 256), bf16),
+            pltpu.VMEM((groups, 8, LOW, 256), bf16),
+            pltpu.VMEM((groups, 8, LOW, 256), bf16),
+            pltpu.VMEM((groups, 8, RANK, 256), bf16),
+            pltpu.VMEM((groups, 4, 2, TOK, 256), bf16),
+            pltpu.VMEM((groups, 4, TOK, 256), bf16),
+            pltpu.VMEM((groups, 4, TOK, 256), bf16),
+            pltpu.VMEM((groups, TOK, 256), f32),
+            pltpu.VMEM((2 * groups, 8, 16, 256), f32),
+            pltpu.VMEM((groups * GRP, SLOT, 256), bf16),
+            pltpu.VMEM((32, SLOT, 256), bf16),
+            pltpu.VMEM((32, SLOT, 256), bf16),
+            pltpu.VMEM((256, TOK), bf16),
         ]
-        + [dma((13,)), dma((rings, 13)), dma((rings, 13)), dma((4, 40)), dma((4, 40))]
-        + [dma((GROUPS, 10)), dma((GROUPS, 10)), dma((2 * GROUPS, 7)), dma((2 * GROUPS, 7))],
+        + [dma((15,)), dma((rings, 13)), dma((rings, 13)), dma((4, 40)), dma((4, 40))]
+        + [dma((groups, 10)), dma((groups, 10)), dma((2 * groups, 7)), dma((2 * groups, 7))]
+        + [dma((15,)), dma((15,))],
+        input_output_aliases={6: 0},
         compiler_params=pltpu.CompilerParams(
-            collective_id=2, has_side_effects=True, vmem_limit_bytes=67043328
+            collective_id=groups, has_side_effects=True, vmem_limit_bytes=67043328
         ),
         name="wave",
-    )(table, vectors, toks, *base_weights, *stores)
+    )(start, table, *vectors, out, toks, *base_weights, *stores)
 
 
 def shards(
@@ -683,31 +684,25 @@
     rank = jnp.sum(same.astype(i32), axis=1)
     near = jnp.sum((same & (n[None, :] // REQ_COL == n[:, None] // REQ_COL)).astype(i32), axis=1)
     waves = (jnp.max(rank) + K) // K
-    most = -(-32 // K)
-    slots = jnp.arange(most * K, dtype=i32)
     mine = owner == col
-    hit = mine[None, :] & (rank[None, :] == slots[:, None])
-    facts = jnp.stack([n, local, length - 1])
-    table = jnp.sum(jnp.where(hit[None], facts[:, None, :], 0), axis=2)
-    table = table + jnp.array([[0], [0], [1]], i32)
-    pair = jnp.arange(32, dtype=i32)
-    out_hit = mine[None, :] & ((n // REQ_COL * 2 + near)[None, :] == pair[:, None])
-    out_slot = jnp.sum(jnp.where(out_hit, rank[None, :], 0), axis=1)
-    home_n = col * REQ_COL + jnp.arange(REQ_COL, dtype=i32)
-    home_hit = home_n[:, None] == n[None, :]
-    home_from = jnp.sum(jnp.where(home_hit, (owner * 2 + near)[None, :], 0), axis=1)
-    tail = [lax.dynamic_slice_in_dim(v, row * 256, 256, 0) for v in (first_shift, second_gain, second_shift)]
-    vectors = jnp.stack([first_gain] + tail)
+    own_rank = jnp.where(mine, rank, -1)
+    source = owner * 2 + near
+    keys = [own_rank] * 3 + [jnp.where(mine, n // REQ_COL * 2 + near, -1), n, n]
+    facts = [n, local, length - 1, rank, source, rank]
+    spots = jnp.arange(64, dtype=i32)[None, :]
+    spots = spots + col * jnp.array([[0], [0], [0], [0], [REQ_COL], [REQ_COL]], i32)
+    hit = jnp.stack(keys)[:, None, :] == spots[:, :, None]
+    table = jnp.sum(jnp.where(hit, jnp.stack(facts)[:, None, :], 0), axis=2)
+    table = table + jnp.array([[0], [0], [1], [0], [0], [0]], i32)
+    vectors = [v[None, :] for v in (first_gain, first_shift, second_gain, second_shift)]
     base_weights = (attention_qkv_weight, attention_out_weight, widen_weight, contract_weight)
 
-    def wave(w, held):
-        with_start = jnp.concatenate([table, jnp.full((1, most * K), w * K, i32)])
-        result = run_wave(with_start, vectors, tok_all, base_weights, stores)
-        return lax.dynamic_update_index_in_dim(held, result, w, 0)
-
-    held = lax.fori_loop(0, waves, wave, jnp.zeros((most, K * SLOT, 256), bf16))
-    packed = jnp.take(held.reshape(most * K, SLOT, 256), out_slot, axis=0)
-    return send_home(packed.reshape(16, 2, SLOT, 256), home_from).reshape(D, TOK)
+    def wave(w, out):
+        start = (w * K).astype(i32)[None]
+        return run_wave(K // GRP, start, table, vectors, out, tok_all, base_weights, stores)
+
+    out = lax.fori_loop(0, waves, wave, jnp.zeros((8, 256, TOK), bf16))
+    return out.reshape(D, TOK)
 
 
 def solution(mesh):

time: 216 us -> 196 us (0.907)
  Pallas kernels: 191 us -> 181 us
  local copies, waits for them, and re-layouts: 14 us -> 6.09 us
  other arithmetic: 8.69 us -> 5 us
    pallas_call x2 -> x1, Pallas kernels: 170 us -> 160 us  [run_wave(): pl.pallas_call(functools.partial(wave_kernel, groups), out_shape=jax.Shap...]
    dynamic_slice x3 -> x0, local copies, waits for them, and re-layouts: 2.28 us -> none  [shards(): lax.dynamic_slice_in_dim(v, row * 256, 256, 0)]
    unnamed x8 -> x4, local copies, waits for them, and re-layouts: 4.52 us -> 3.93 us
where the time goes in v4:
time: 196 us; the launch traced here: 193 us
  Pallas kernels  181 us (92%)
  local copies, waits for them, and re-layouts  6.09 us (3%)
  other arithmetic  5 us (3%)
    pallas_call x1, Pallas kernels, run_wave(): pl.pallas_call(functools.partial(wave_kernel, groups), out_shape=jax.Shap...  160 us
    pallas_call x1, Pallas kernels, entry_gather(): pl.pallas_call(entry_kernel, out_shape=[jax.ShapeDtypeStruct((16,) + a.sh...  20.9 us
    unnamed x4, local copies, waits for them, and re-layouts  3.93 us

profile of v4, /device:TPU:1, one launch (start us, length us, event | category | flops | bytes accessed | tf_op | source)
XLA Modules:
  0.0 193.1 jit_solution(4025969753006152881)
XLA Ops:
  0.0 0.7 multiply_bitcast_fusion
  0.7 0.9 select_reduce_fusion.1
  1.5 0.8 scatter.9.meta_ref
  2.3 0.0 copy-start
  2.3 0.1 iota_add_fusion
  2.4 1.7 copy.26
  4.1 0.0 copy-done
  4.1 20.9 %entry_gather.1 = (bf16[16,256,256]{2,1,0:T(8,128)(2,1)}, s32[16,8,128]{2,1,0:T(8,128)}) custom-call(bf16[256,256]{1,0:T(8,128)(2,1)} %bitcast.22, s32[8,128]{1,0:T(8,128)} %copy-done), custom_call_target="tpu_custom_call" | custom-call | tf_op jit(solution)/shard_map/entry_gather/pallas_call | solution.py:249
  24.9 1.0 add_reduce_fusion
  25.9 0.1 sub.38
  26.0 0.1 reshape_squeeze.6
  26.1 0.1 reshape_squeeze.7
  26.2 0.2 convert_reduce_fusion
  26.4 0.6 reduce_max.9
  27.8 0.3 select_reduce_fusion
  28.1 1.3 broadcast_add_fusion
  29.4 1.1 broadcast_in_dim.59
  30.4 160.4 %while.12 = (s32[]{:T(128)}, bf16[8,256,256]{2,1,0:T(8,128)(2,1)}, s32[]{:T(128)}, s32[6,64]{1,0:T(8,128)}, f32[1,256]{1,0:T(1,128)}, /*index=5*/f32[1,2048]{1,0...) while((s32[]{:T(128)}, bf16[8,256,256]{2,1,0:T(8,128)(2,1)}, ...), condition=%wide.region_6.7_spmd, body=%wide.region_5.6_spmd.sunk | while | flops 3 | bytes 217 | solution.py:704
  30.4 160.4 %wave.1 = bf16[8,256,256]{2,1,0:T(8,128)(2,1)} custom-call(s32[1]{0:T(128)} %bitcast.19.refs_0_, s32[6,64]{1,0:T(8,128)} %get-tuple-element.373.refs_1_, f32[1,256]{1,0:T(1,128)} %get-tuple-element.374.refs_2_, f32[1,2048]{1,0:T(1,128)} %get-tuple-element.375.refs_3_, f32[1,2048]{1,0:T(1,128)} %get-tuple-element.376.refs_4_, ...), custom_call_target="tpu_custom_call", output_to_operand_aliasing={{}: (6, {})} | custom-call | tf_op jit(solution)/shard_map/while/body/wave/pallas_call | solution.py:618
  190.8 2.3 %copy.38 = bf16[2048,256]{1,0:T(8,128)(2,1)} copy(bf16[2048,256]{1,0:T(8,128)(2,1)} %bitcast.21) | data formatting | bytes 2097152
  (8 shorter events, 0.1 us)
Async XLA Ops:
  2.3 1.7 copy-start
